TPU v7x, 32 devices: a whole 2x2x4 slice. The times are simulated.
32 devices in a mesh: sub: 4 (over x, core), beam: 4 (over z), comp: 2 (over y).
Axes of the slice: x: 2, y: 2, z: 4, core: 2. Of those that a mesh axis runs over, the one named last changes fastest.
Arguments:
- raw_pulses: bfloat16 [4096, 2, 16384], P(('sub', 'beam', 'comp')), may hold values from -6 to 6
- range_filter: float32 [2, 16384], replicated, may hold values from -4 to 4
- steer_angle: float32 [64, 4096], P(None, ('sub', 'beam', 'comp')), may hold values from -3.140625 to 3.140625
- band_offsets: int32 [2, 384], P(None, ('beam', 'comp')), may hold values from -4 to 12, as said below
- band_weights: float32 [2, 384, 8], P(None, ('beam', 'comp')), may hold values from -1.5 to 1.5
- beam_delay: float32 [2, 384], P(None, ('beam', 'comp')), may hold values from -3 to 3
Outputs:
- scene_beams: float32 [256, 2, 16384], P(('beam', 'comp'), None, 'sub')
Inputs may be any that keep to these rules, and one draw needn't show every extreme that they name: `band_offsets`: for new beam u of a merge level l and a block (0 <= u < 2 * 8 2^l), each side's offset is u // 2 - 8 // 2 + 1 or one less; the first beam of every level and block takes the lesser value, the last the greater.
All inputs are finite; a program needn't handle non-finite values.
Results may differ from a plain program's by a relative error of at most 0.0059.
Values may be sent and summed in bfloat16 or wider, within the bound.
A program may use at most 128 MiB of HBM per device.

v0:
```python
import functools
import math

import jax
import jax.numpy as jnp
from jax import lax
from jax.experimental import pallas as pl
from jax.experimental.pallas import tpu as pltpu
from jax.sharding import PartitionSpec as P

NR = 16384
RADIX = 128
BAND = 8
CHUNKS = 16
COMP_FIRST = CHUNKS
LAG = 3
MESH = pl.DeviceIdType.MESH


def dft_table(length):
    index_row = jnp.arange(length, dtype=jnp.int32)
    product = index_row[:, None] * index_row[None, :] % length
    phase_angle = product.astype(jnp.float32) * (2.0 * math.pi / length)
    return (jnp.cos(phase_angle).astype(jnp.bfloat16), (-jnp.sin(phase_angle)).astype(jnp.bfloat16))


def real_form(length):
    cos_part, sin_part = dft_table(length)
    upper_rows = jnp.concatenate([cos_part, sin_part], axis=1)
    lower_rows = jnp.concatenate([-sin_part, cos_part], axis=1)
    return jnp.concatenate([upper_rows, lower_rows], axis=0)


def twiddle():
    freq_index = jnp.arange(RADIX, dtype=jnp.int32)[:, None]
    time_index = jnp.arange(RADIX, dtype=jnp.int32)[None, :]
    phase_angle = (freq_index * time_index % NR).astype(jnp.float32) * (2.0 * math.pi / NR)
    return (jnp.cos(phase_angle), -jnp.sin(phase_angle))


def compress(beams, range_filter):
    number = beams.shape[1]
    samples = beams.reshape(2, number, RADIX, RADIX)
    first = real_form(RADIX).reshape(2, RADIX, 2, RADIX)
    section_one = jnp.einsum("rpan,rask->spkn", samples, first, preferred_element_type=jnp.float32)
    cos_part, sin_part = twiddle()
    real_in = section_one[0]
    imag_in = section_one[1]
    turned = jnp.stack(
        [real_in * cos_part - imag_in * sin_part, real_in * sin_part + imag_in * cos_part], 0
    )
    high = turned.astype(jnp.bfloat16)
    low = (turned - high.astype(jnp.float32)).astype(jnp.bfloat16)
    spectrum = jnp.einsum("rpkn,rnsm->spmk", high, first, preferred_element_type=jnp.float32)
    spectrum += jnp.einsum("rpkn,rnsm->spmk", low, first, preferred_element_type=jnp.float32)
    spectrum = spectrum.reshape(2, number, NR)
    factor = NR ** (-0.5)
    real_out = (spectrum[0] * range_filter[0] - spectrum[1] * range_filter[1]) * factor
    imag_out = (spectrum[0] * range_filter[1] + spectrum[1] * range_filter[0]) * factor
    return jnp.stack([real_out, imag_out], 0)


def steering(phase_angle, factor):
    real_part = (jnp.cos(phase_angle) * factor).astype(jnp.bfloat16)
    imag_part = (jnp.sin(phase_angle) * factor).astype(jnp.bfloat16)
    upper_rows = jnp.stack([real_part, -imag_part], -1).reshape(phase_angle.shape[0], -1)
    lower_rows = jnp.stack([imag_part, real_part], -1).reshape(phase_angle.shape[0], -1)
    return jnp.concatenate([upper_rows, lower_rows], 0)


def reduce_kernel(
    beam_count, comp_count, comp_chunks, weight_ref, raw_ref, out_ref, raw, part, recv_one,
    send_two, recv_two, load_sem, one_send, one_recv, two_send, two_recv,
):
    sizes = {"beam": beam_count, "comp": comp_count}
    mine = {"beam": lax.axis_index("beam"), "comp": lax.axis_index("comp")}
    rows = out_ref.shape[1]
    width = raw_ref.shape[-1] // CHUNKS
    loads = []
    for j in range(CHUNKS):
        cols = pl.ds(j * width, width)
        loads.append(
            pltpu.make_async_copy(raw_ref.at[:, :, cols], raw.at[:, :, cols], load_sem.at[j])
        )
        loads[j].start()

    def peer_of(axis, d):
        return lax.rem(mine[axis] + d, sizes[axis])

    def route(j):
        beams_before = j * (CHUNKS - comp_chunks) // CHUNKS
        beams_after = (j + 1) * (CHUNKS - comp_chunks) // CHUNKS
        return ("beam", "comp") if beams_after > beams_before else ("comp", "beam")

    def owned(ref, axis, index, cols):
        if axis == "comp":
            return ref[:, :, index, :, cols]
        return ref[:, index, :, :, cols]

    barrier = pltpu.get_barrier_semaphore()
    for axis in sizes:
        for d in range(1, sizes[axis]):
            pl.semaphore_signal(
                barrier, inc=1, device_id={axis: peer_of(axis, d)}, device_id_type=MESH
            )
    pl.semaphore_wait(barrier, comp_count + beam_count - 2)
    first = []
    second = []

    def start_first(j):
        cols = pl.ds(j * width, width)
        loads[j].wait()
        pulses = raw[:, :, cols].reshape(-1, width)
        product = jnp.dot(weight_ref[...], pulses, preferred_element_type=jnp.float32)
        part[:, :, :, :, cols] = product.astype(jnp.bfloat16).reshape(
            2, beam_count, comp_count, rows, width
        )
        axis, other = route(j)
        group = []
        for d in range(1, sizes[axis]):
            peer = peer_of(axis, d)
            source = (
                part.at[:, :, peer, :, cols] if axis == "comp" else part.at[:, peer, :, :, cols]
            )
            copy = pltpu.make_async_remote_copy(
                src_ref=source,
                dst_ref=recv_one.at[d - 1, :, pl.ds(0, sizes[other]), :, cols],
                send_sem=one_send.at[d - 1, j],
                recv_sem=one_recv.at[d - 1, j],
                device_id={axis: peer},
                device_id_type=MESH,
            )
            copy.start()
            group.append(copy)
        first.append(group)

    def start_second(j):
        cols = pl.ds(j * width, width)
        axis, other = route(j)
        for copy in first[j]:
            copy.wait_recv()
        total = owned(part, axis, mine[axis], cols).astype(jnp.float32)
        for d in range(1, sizes[axis]):
            total += recv_one[d - 1, :, : sizes[other], :, cols].astype(jnp.float32)
        send_two[:, : sizes[other], :, cols] = total.astype(jnp.bfloat16)
        group = []
        for d in range(1, sizes[other]):
            peer = peer_of(other, d)
            copy = pltpu.make_async_remote_copy(
                src_ref=send_two.at[:, peer, :, cols],
                dst_ref=recv_two.at[d - 1, :, :, cols],
                send_sem=two_send.at[d - 1, j],
                recv_sem=two_recv.at[d - 1, j],
                device_id={other: peer},
                device_id_type=MESH,
            )
            copy.start()
            group.append(copy)
        second.append(group)

    for j in range(CHUNKS + LAG):
        if j < CHUNKS:
            start_first(j)
        if j >= LAG:
            start_second(j - LAG)
    for j in range(CHUNKS):
        cols = pl.ds(j * width, width)
        axis, other = route(j)
        for copy in second[j]:
            copy.wait_recv()
        total = part[:, mine["beam"], mine["comp"], :, cols].astype(jnp.float32)
        for d in range(1, sizes[axis]):
            total += recv_one[d - 1, :, mine[other], :, cols].astype(jnp.float32)
        for d in range(1, sizes[other]):
            total += recv_two[d - 1, :, :, cols].astype(jnp.float32)
        out_ref[:, :, cols] = total.astype(jnp.bfloat16)
    for group in first + second:
        for copy in group:
            copy.wait_send()


def reduce_beams(weights, raw_pulses, beam_count, comp_count):
    blocks = beam_count * comp_count
    rows = weights.shape[0] // (2 * blocks)
    length = raw_pulses.shape[2]
    most = max(beam_count, comp_count)
    return pl.pallas_call(
        functools.partial(reduce_kernel, beam_count, comp_count, COMP_FIRST),
        out_shape=jax.ShapeDtypeStruct((2, rows, length), jnp.bfloat16),
        in_specs=[
            pl.BlockSpec(memory_space=pltpu.VMEM),
            pl.BlockSpec(memory_space=pl.ANY),
        ],
        out_specs=pl.BlockSpec(memory_space=pltpu.VMEM),
        scratch_shapes=[
            pltpu.VMEM(raw_pulses.shape, jnp.bfloat16),
            pltpu.VMEM((2, beam_count, comp_count, rows, length), jnp.bfloat16),
            pltpu.VMEM((most - 1, 2, most, rows, length), jnp.bfloat16),
            pltpu.VMEM((2, most, rows, length), jnp.bfloat16),
            pltpu.VMEM((most - 1, 2, rows, length), jnp.bfloat16),
            pltpu.SemaphoreType.DMA((CHUNKS,)),
            pltpu.SemaphoreType.DMA((most - 1, CHUNKS)),
            pltpu.SemaphoreType.DMA((most - 1, CHUNKS)),
            pltpu.SemaphoreType.DMA((most - 1, CHUNKS)),
            pltpu.SemaphoreType.DMA((most - 1, CHUNKS)),
        ],
        compiler_params=pltpu.CompilerParams(
            collective_id=0, has_side_effects=True, vmem_limit_bytes=60 * 2**20
        ),
    )(weights, raw_pulses)


def band_matrix(offset, weight, span):
    tap_index = offset[:, None] + BAND // 2 + jnp.arange(BAND, dtype=jnp.int32)[None, :]
    matches = tap_index[:, :, None] == jnp.arange(span, dtype=jnp.int32)[None, None, :]
    return jnp.sum(
        jnp.where(matches, weight[:, :, None], jnp.zeros_like(weight)[:, :, None]), axis=1
    )


def exchange_kernel(
    counts, spread, image_ref, out_ref, send_sem, recv_sem, low_send, low_recv, high_send,
    high_recv, own_sem,
):
    sub_count, beam_count, comp_count = counts
    s = lax.axis_index("sub")
    block = lax.axis_index("beam") * comp_count + lax.axis_index("comp")
    has_low = block > 0
    has_high = block < beam_count * comp_count - 1
    width = out_ref.shape[-1]
    hops = sub_count if spread else 1

    def place(d, step):
        target = block + step
        return {
            "sub": lax.rem(s + d, sub_count),
            "beam": lax.div(target, comp_count),
            "comp": lax.rem(target, comp_count),
        }

    def columns(d):
        if not spread:
            return pl.ds(0, width)
        return pl.ds(pl.multiple_of(lax.rem(s + d, sub_count) * width, 128), width)

    barrier = pltpu.get_barrier_semaphore()
    for d in range(1, hops):
        pl.semaphore_signal(barrier, inc=1, device_id=place(d, 0), device_id_type=MESH)

    @pl.when(has_high)
    def _():
        for d in range(hops):
            pl.semaphore_signal(barrier, inc=1, device_id=place(d, 1), device_id_type=MESH)

    @pl.when(has_low)
    def _():
        for d in range(hops):
            pl.semaphore_signal(barrier, inc=1, device_id=place(d, -1), device_id_type=MESH)

    amount = hops - 1 + hops * (has_low.astype(jnp.int32) + has_high.astype(jnp.int32))
    pl.semaphore_wait(barrier, amount)

    def halo(d, step):
        source = slice(None) if not spread else s
        half = 1 if step > 0 else 0
        slot = 0 if step > 0 else out_ref.shape[2] - 1
        target = out_ref.at[:, :, slot] if not spread else out_ref.at[source, :, slot]
        origin = (
            image_ref.at[:, :, half]
            if not spread
            else image_ref.at[:, half, :, columns(d)]
        )
        return pltpu.make_async_remote_copy(
            src_ref=origin,
            dst_ref=target,
            send_sem=(low_send if step > 0 else high_send).at[d],
            recv_sem=(low_recv if step > 0 else high_recv).at[d],
            device_id=place(d, step),
            device_id_type=MESH,
        )

    @pl.when(has_high)
    def _():
        for d in range(hops):
            halo(d, 1).start()

    @pl.when(has_low)
    def _():
        for d in range(hops):
            halo(d, -1).start()

    copies = []
    for d in range(1, hops):
        copy = pltpu.make_async_remote_copy(
            src_ref=image_ref.at[:, :, :, columns(d)],
            dst_ref=out_ref.at[s, :, pl.ds(1, 2)],
            send_sem=send_sem.at[d],
            recv_sem=recv_sem.at[d],
            device_id=place(d, 0),
            device_id_type=MESH,
        )
        copy.start()
        copies.append(copy)
    if spread:
        own = pltpu.make_async_copy(
            image_ref.at[:, :, :, columns(0)], out_ref.at[s, :, pl.ds(1, 2)], own_sem
        )
        own.start()
        copies.append(own)

    low_slot = 0
    high_slot = out_ref.shape[2] - 1
    blank = jnp.zeros(out_ref.shape[:2] + out_ref.shape[3:], out_ref.dtype)

    @pl.when(has_low)
    def _():
        for d in range(hops):
            halo(d, 1).wait_recv()
            halo(d, -1).wait_send()

    @pl.when(jnp.logical_not(has_low))
    def _():
        out_ref[:, :, low_slot] = blank

    @pl.when(has_high)
    def _():
        for d in range(hops):
            halo(d, -1).wait_recv()
            halo(d, 1).wait_send()

    @pl.when(jnp.logical_not(has_high))
    def _():
        out_ref[:, :, high_slot] = blank

    for copy in copies:
        copy.wait()


def exchange(image, shape, counts, spread, kernel_id):
    hops = counts[0] if spread else 1
    return pl.pallas_call(
        functools.partial(exchange_kernel, counts, spread),
        out_shape=jax.ShapeDtypeStruct(shape, jnp.bfloat16),
        in_specs=[pl.BlockSpec(memory_space=pltpu.VMEM)],
        out_specs=pl.BlockSpec(memory_space=pltpu.VMEM),
        scratch_shapes=[pltpu.SemaphoreType.DMA((hops,))] * 6 + [pltpu.SemaphoreType.DMA],
        compiler_params=pltpu.CompilerParams(
            collective_id=kernel_id, has_side_effects=True, vmem_limit_bytes=24 * 2**20
        ),
    )(image)


def phases(delay, start, width):
    coarse_row = (start + RADIX * jnp.arange(width // RADIX, dtype=jnp.int32)).astype(jnp.float32)
    coarse = delay[..., None] * (1.0 + coarse_row / NR)
    fine = delay[..., None] * (jnp.arange(RADIX, dtype=jnp.float32) / NR)
    cos_one, sin_one = jnp.cos(coarse)[..., None], jnp.sin(coarse)[..., None]
    cos_two, sin_two = jnp.cos(fine)[..., None, :], jnp.sin(fine)[..., None, :]
    cosine = cos_one * cos_two - sin_one * sin_two
    sine = sin_one * cos_two + cos_one * sin_two
    shape = delay.shape + (width,)
    return cosine.reshape(shape), sine.reshape(shape)


def merge(window, offset, weight, cosine, sine):
    groups, span, width = window.shape[0] // 2, window.shape[2], window.shape[3]
    paired = window.reshape(groups, 2, 2, span, width)
    real_sum, imag_sum = 0.0, 0.0
    for c in range(2):
        matrix = band_matrix(offset[c], weight[c], span)
        high = matrix.astype(jnp.bfloat16)
        low = (matrix - high.astype(jnp.float32)).astype(jnp.bfloat16)
        both = jnp.concatenate([high, low], axis=0)
        blended = jnp.einsum(
            "jw,gpwr->gpjr", both, paired[:, c], preferred_element_type=jnp.float32
        )
        count = matrix.shape[0]
        blended = blended[:, :, :count] + blended[:, :, count:]
        real_sum += cosine[c] * blended[:, 0] - sine[c] * blended[:, 1]
        imag_sum += sine[c] * blended[:, 0] + cosine[c] * blended[:, 1]
    return real_sum, imag_sum


def body(raw_pulses, range_filter, steer_angle, band_offsets, band_weights, beam_delay):
    sub_count = lax.axis_size("sub")
    beam_devices = lax.axis_size("beam")
    comp_devices = lax.axis_size("comp")
    counts = (sub_count, beam_devices, comp_devices)
    blocks = beam_devices * comp_devices
    factor = float(raw_pulses.shape[0] * blocks) ** (-0.5)
    first_beams = steer_angle.shape[0] // blocks
    levels = sub_count.bit_length() - 1
    margin = BAND // 2
    width = NR // sub_count
    start = lax.axis_index("sub") * width
    cosine, sine = phases(beam_delay, start, width)
    weights = steering(steer_angle, factor)
    summed = reduce_beams(weights, raw_pulses, beam_devices, comp_devices)
    image = compress(summed, range_filter).astype(jnp.bfloat16)
    image = image.reshape(2, first_beams // margin, margin, NR)
    window = exchange(image, (sub_count, 2, 4, margin, width), counts, True, 1)
    window = window.reshape(sub_count, 2, 4 * margin, width)
    beam_count = first_beams
    for level_index in range(levels):
        base = first_beams * (2 ** (level_index + 1) - 2)
        cols = slice(base, base + 2 * beam_count)
        real, imag = merge(
            window, band_offsets[:, cols], band_weights[:, cols], cosine[:, cols], sine[:, cols]
        )
        beam_count *= 2
        if level_index + 1 < levels:
            image = jnp.stack([real, imag], 1).astype(jnp.bfloat16)
            groups = image.shape[0]
            ends = jnp.stack([image[:, :, :margin], image[:, :, -margin:]], 2)
            edges = exchange(
                ends, (groups, 2, 2, margin, width), counts, False, 2 + level_index
            )
            window = jnp.concatenate([edges[:, :, 0], image, edges[:, :, 1]], 2)
    return jnp.stack([real[0], imag[0]], 1)


def solution(mesh):
    in_specs = (
        P(("sub", "beam", "comp"), None, None),
        P(),
        P(None, ("sub", "beam", "comp")),
        P(None, ("beam", "comp")),
        P(None, ("beam", "comp"), None),
        P(None, ("beam", "comp")),
    )
    out_specs = P(("beam", "comp"), None, "sub")
    return jax.shard_map(body, mesh=mesh, in_specs=in_specs, out_specs=out_specs, check_vma=False)
```

profile of v0, /device:TPU:0, one launch (start us, length us, event | category | flops | bytes accessed | tf_op | source)
XLA Modules:
  0.0 108.3 jit_solution(7890050611976434907)
XLA Ops:
  0.0 0.8 add_bitcast_fusion.2
  0.9 0.8 add_bitcast_fusion.5
  1.6 0.8 slice_bitcast_fusion.18
  2.5 0.7 slice_bitcast_fusion.21
  3.8 0.9 negate_bitcast_fusion
  4.9 0.9 fusion.28
  6.3 0.6 pad_maximum_fusion.5.weight_ref
  6.9 0.3 negate_convert_fusion
  8.1 0.3 sine_negate_fusion
  8.3 60.2 %shard_map.64 = bf16[2,8,16384]{2,1,0:T(8,128)(2,1)} custom-call(bf16[128,256]{1,0:T(8,128)(2,1)} %pad_maximum_fusion.5.weight_ref, bf16[128,2,16384]{2,1,0:T(2,128)(2,1)} %raw_ref.1), custom_call_target="tpu_custom_call" | custom-call | tf_op jit(solution)/shard_map/pallas_call | solution.py:187
  68.5 1.3 %convolution_bitcast_fusion.6 = f32[2,8,128,128]{3,2,1,0:T(8,128)S(1)} fusion(bf16[2,128,2,128,1]{1,3,0,4,2:T(8,128)(2,1)S(1)} %copy.66, bf16[2,8,128,128]{3,1,2,0:T(8,128)(2,1)} %bitcast.163), kind=kOutput, calls=%fused_computation.8 | convolution fusion | flops 134217728 | bytes 1703936 | tf_op jit(solution)/shard_map/rpan,rask->spkn/dot_general | solution.py:45
  70.0 0.3 convolution_bitcast_fusion.4
  70.4 0.3 fusion.1
  71.2 0.3 multiply_convert_fusion.1
  71.6 0.4 pad_maximum_fusion.2.image_ref
  72.0 16.1 %shard_map.65 = bf16[4,2,4,4,4096]{4,3,2,1,0:T(4,128)(2,1)S(1)} custom-call(bf16[2,2,4,16384]{3,2,1,0:T(4,128)(2,1)S(1)} %pad_maximum_fusion.2.image_ref), custom_call_target="tpu_custom_call" | custom-call | tf_op jit(solution)/shard_map/pallas_call | solution.py:341
  88.0 0.3 reshape_reshape.3
  88.3 0.5 convolution_bitcast_fusion.3
  88.9 1.1 %slice_add_fusion.3 = f32[2,2,16,4096]{3,2,1,0:T(8,128)} fusion(f32[2,2,32,4096]{3,2,1,0:T(8,128)S(1)} %convolution_bitcast_fusion.3), kind=kLoop, calls=%fused_computation.14 | loop fusion | flops 262144 | bytes 3145728 | tf_op jit(solution)/shard_map/add | solution.py:378
  90.0 0.5 convolution_bitcast_fusion.2
  90.5 1.1 slice_add_fusion.2
  91.6 1.9 %multiply_subtract_fusion = (f32[2,48,32,128]{3,2,1,0:T(8,128)S(1)}, f32[2,48,32,128]{3,2,1,0:T(8,128)}) fusion(f32[2,48,128]{2,1,0:T(8,128)S(1)} %get-tuple-element.46, f32[2,48,32]{2,1,0:T(8,128)S(1)} %get-tuple-element.44, f32[2,48,128]{2,1,0:T(8,128)S(1)} %get-tuple-element.45, f32[2,48,32]{2,1,0:T(8,128)S(1)} %get-tuple-element.43), kind=kLoop, calls=%fused_computation.5 | loop fusion | flops 2359296 | bytes 3268608 | tf_op jit(solution)/shard_map/sub | solution.py:359
  93.5 0.3 sub.52
  93.7 1.6 %add.246 = f32[2,48,4096]{2,1,0:T(8,128)S(1)} reshape(f32[2,48,32,128]{3,2,1,0:T(8,128)} %get-tuple-element.32) | data formatting | bytes 3145728 | tf_op jit(solution)/shard_map/add | solution.py:360
  95.4 1.1 %copy-done = f32[2,2,16,4096]{3,2,1,0:T(8,128)S(1)} copy-done((f32[2,2,16,4096]{3,2,1,0:T(8,128)S(1)}, f32[2,2,16,4096]{3,2,1,0:T(8,128)}, u32[]{:S(2)}) %copy-start) | copy-done | bytes 1048600
  96.5 0.3 copy-done.1
  97.4 7.0 %shard_map.66 = bf16[2,2,2,4,4096]{4,3,2,1,0:T(4,128)(2,1)S(1)} custom-call(bf16[2,2,2,4,4096]{4,3,2,1,0:T(4,128)(2,1)S(1)} %pad_maximum_fusion.3.image_ref), custom_call_target="tpu_custom_call" | custom-call | tf_op jit(solution)/shard_map/pallas_call | solution.py:341
  104.5 0.3 maximum_bitcast_fusion
  104.8 0.5 convolution_bitcast_fusion
  105.5 0.5 convolution_bitcast_fusion.1
  106.2 0.3 add_bitcast_fusion.1
  106.5 1.8 %copy.63 = f32[32,2,4096]{2,1,0:T(2,128)} copy(f32[32,2,4096]{2,0,1:T(8,128)S(1)} %pad_maximum_fusion.1) | data formatting | bytes 2097152 | tf_op jit(solution)/shard_map/stack | solution.py:419
  (46 shorter events, 3.8 us)
Async XLA Ops:
  0.0 7.4 %copy-start.3 = (f32[2,48]{1,0:T(2,128)S(1)}, f32[2,48]{1,0:T(2,128)}, u32[]{:S(2)}) copy-start(f32[2,48]{1,0:T(2,128)} %param.11) | copy-start | bytes 1156
  0.0 7.9 %copy-start.2 = (f32[2,16384]{1,0:T(2,128)S(1)}, f32[2,16384]{1,0:T(2,128)}, u32[]{:S(2)}) copy-start(f32[2,16384]{1,0:T(2,128)} %param.7) | copy-start | bytes 393220
  95.3 1.2 %copy-start = (f32[2,2,16,4096]{3,2,1,0:T(8,128)S(1)}, f32[2,2,16,4096]{3,2,1,0:T(8,128)}, u32[]{:S(2)}) copy-start(f32[2,2,16,4096]{3,2,1,0:T(8,128)} %slice_add_fusion.3) | copy-start | bytes 3145732
  95.3 1.5 %copy-start.1 = (f32[2,2,16,4096]{3,2,1,0:T(8,128)S(1)}, f32[2,2,16,4096]{3,2,1,0:T(8,128)}, u32[]{:S(2)}) copy-start(f32[2,2,16,4096]{3,2,1,0:T(8,128)} %slice_add_fusion.2) | copy-start | bytes 3145732
where the time goes:
time: 110 us; the launch traced here: 108 us
  Pallas kernels  83.2 us (76%)
  other arithmetic  12 us (11%)
  local copies, waits for them, and re-layouts  8.49 us (8%)
  matrix products  4.19 us (4%)
    pallas_call x1, Pallas kernels, reduce_beams(): pl.pallas_call(functools.partial(reduce_kernel, beam_count, comp_count, C...  60.2 us
    pallas_call x2, Pallas kernels, exchange(): pl.pallas_call(functools.partial(exchange_kernel, counts, spread), out_sh...  23.1 us
    add x4, other arithmetic, merge(): blended = blended[:, :, :count] + blended[:, :, count:]  2.4 us

commit v1 on v0

v1 whole, which is shorter than its diff:
```python
import functools
import itertools
import math

import jax
import jax.numpy as jnp
import numpy as np
from jax import lax
from jax.experimental import pallas as pl
from jax.experimental.pallas import tpu as pltpu
from jax.sharding import PartitionSpec as P

BAND = 8
EXTRA = 8
FIELDS = 16
GROUP = 4
PIECES = 8
LAG = 3
LAG_TWO = 2
OUT_PIECES = 4
MESH = pl.DeviceIdType.MESH
F32 = jnp.float32
BF16 = jnp.bfloat16


def dft_table(length):
    index_row = np.arange(length, dtype=np.int32)
    product = index_row[:, None] * index_row[None, :] % length
    phase_angle = product.astype(np.float32) * np.float32(2.0 * math.pi / length)
    return np.cos(phase_angle).astype(BF16), (-np.sin(phase_angle)).astype(BF16)


def real_form(length):
    cos_part, sin_part = dft_table(length)
    upper_rows = np.concatenate([cos_part, sin_part], axis=1)
    lower_rows = np.concatenate([-sin_part, cos_part], axis=1)
    return np.concatenate([upper_rows, lower_rows], axis=0)


def twiddle(radix):
    index_row = np.arange(radix, dtype=np.int32)
    product = index_row[:, None] * index_row[None, :] % (radix * radix)
    phase_angle = product.astype(np.float32) * np.float32(2.0 * math.pi / (radix * radix))
    return np.stack([np.cos(phase_angle), -np.sin(phase_angle)], 0).astype(np.float32)


def split(value):
    high = value.astype(BF16)
    return high, (value - high.astype(F32)).astype(BF16)


def dot(a, b):
    return jnp.dot(a, b, preferred_element_type=F32)


class Plan:
    def __init__(self, counts, angle_shape, length, columns):
        self.sub, self.beam, self.comp = counts
        self.blocks = self.beam * self.comp
        self.beams, self.pulses = angle_shape
        self.first = self.beams // self.blocks
        self.length = length
        self.radix = math.isqrt(length)
        self.columns = columns
        self.group = min(GROUP, self.first)
        self.groups = self.first // self.group
        self.rows = 2 * self.group
        self.width = length // PIECES
        self.levels = self.sub.bit_length() - 1
        self.quarter = self.radix // self.sub
        self.share = self.quarter // self.comp
        self.outs = self.first * self.sub
        self.padded = -(-2 * columns // 128) * 128
        self.slots = self.comp + 2
        self.factor = float(self.pulses * self.blocks) ** (-0.5)
        self.sizes = []
        for level in range(self.levels):
            own = self.comp * self.first * 2 ** (level + 1)
            self.sizes.append(own + (0 if level == self.levels - 1 else 2 * EXTRA))
        self.depths = [2 * self.slots * self.first] + [2 * n for n in self.sizes[:-1]]
        near = {(0, d, e) for d in (-1, 0, 1) for e in range(self.comp)}
        near |= {(d, 0, e) for d in range(self.sub) for e in range(self.comp)}
        near |= {(0, d, 0) for d in range(self.beam)}
        self.peers = sorted({(d % self.sub, e % self.beam, f % self.comp) for d, e, f in near} - {(0, 0, 0)})
        self.table_peers = [
            (d, e)
            for d in (-1, 0, 1)
            for e in range(self.comp)
            if (d % self.beam, e) != (0, 0)
        ]
        self.swap_peers = [
            (d, e) for d in range(self.sub) for e in range(self.comp) if (d, e) != (0, 0)
        ]

    def pieces(self, level):
        new = self.first * 2 ** (level + 1)
        inner = [(k, 0, new) for k in range(self.comp)]
        if level == self.levels - 1:
            return inner
        return [(-1, new - EXTRA, EXTRA)] + inner + [(self.comp, 0, EXTRA)]


def fused_kernel(
    plan, angle_ref, raw_hbm, filter_hbm, table_ref, first_hbm, second_hbm, turn_hbm, out_ref,
    raw, weight, part, recv_one, held, recv_two, swap, first, second, turn, filt, blend, image,
    window, tables, fields, *rest,
):
    p = plan
    levels = p.levels
    lhs = rest[:levels]
    delay = rest[levels : 2 * levels]
    phase = rest[2 * levels : 3 * levels]
    (final, outbound, inbound, load_sem, const_sem, table_send, table_recv, one_send, one_recv,
     two_send, two_recv, swap_send, swap_recv, halo_send, halo_recv, out_send, out_recv) = rest[
        3 * levels :
    ]
    s = lax.axis_index("sub")
    b = lax.axis_index("beam")
    c = lax.axis_index("comp")
    has_low = b > 0
    has_high = b < p.beam - 1
    radix = p.radix

    def at(ds, db, dc):
        return {
            "sub": lax.rem(s + (ds % p.sub), p.sub),
            "beam": lax.rem(b + (db % p.beam), p.beam),
            "comp": lax.rem(c + (dc % p.comp), p.comp),
        }

    def remote(source, target, send, recv, place):
        return pltpu.make_async_remote_copy(
            src_ref=source, dst_ref=target, send_sem=send, recv_sem=recv, device_id=place,
            device_id_type=MESH,
        )

    loads = []
    for h in range(PIECES):
        cols = pl.ds(h * p.width, p.width)
        loads.append(
            pltpu.make_async_copy(raw_hbm.at[:, :, cols], raw.at[:, :, cols], load_sem.at[h])
        )
        loads[h].start()
    constants = [
        pltpu.make_async_copy(source, target, const_sem.at[i])
        for i, (source, target) in enumerate(
            [(first_hbm, first), (second_hbm, second), (turn_hbm, turn), (filter_hbm, filt)]
        )
    ]
    for copy in constants:
        copy.start()

    barrier = pltpu.get_barrier_semaphore()
    for place in p.peers:
        pl.semaphore_signal(barrier, inc=1, device_id=at(*place), device_id_type=MESH)

    angle = angle_ref[...]
    cos_part = (jnp.cos(angle) * p.factor).astype(BF16)
    sin_part = (jnp.sin(angle) * p.factor).astype(BF16)
    stacked = jnp.concatenate(
        [
            jnp.concatenate([cos_part, -sin_part], axis=1),
            jnp.concatenate([sin_part, cos_part], axis=1),
        ],
        axis=0,
    )
    count, deep = 2 * p.beams, 2 * p.pulses
    source = lax.broadcasted_iota(jnp.int32, (deep, deep), 0)
    target = lax.broadcasted_iota(jnp.int32, (deep, deep), 1)
    place = jnp.where(source < p.pulses, 2 * source, 2 * (source - p.pulses) + 1)
    spread = jnp.where(place == target, 1.0, 0.0).astype(BF16)
    target = lax.broadcasted_iota(jnp.int32, (count, count), 0)
    source = lax.broadcasted_iota(jnp.int32, (count, count), 1)

    def bits(value, size):
        return jnp.bitwise_and(value, size - 1), lax.shift_right_logical(
            value, jnp.full_like(value, size.bit_length() - 1)
        )

    within, upper = bits(target, p.group)
    half, upper = bits(upper, 2)
    beam_at, upper = bits(upper, p.beam)
    comp_at, group_at = bits(upper, p.comp)
    origin = half * p.beams + (
        (beam_at * p.comp + comp_at) * p.first + group_at * p.group + within
    )
    order = jnp.where(origin == source, 1.0, 0.0).astype(BF16)
    weight[...] = dot(order, dot(stacked, spread).astype(BF16)).astype(BF16)

    pl.semaphore_wait(barrier, len(p.peers))

    started = []
    table_copies = []

    def table_copy(i, db, dc):
        return remote(
            table_ref,
            tables.at[1 - db, lax.rem(c + p.comp, p.comp)],
            table_send.at[i], table_recv.at[i], at(0, db, dc),
        )

    for i, (db, dc) in enumerate(p.table_peers):
        copy = table_copy(i, db, dc)
        copy.start()
        table_copies.append(copy)

    def columns_of(h):
        return pl.ds(h * p.width, p.width)

    one, two, swaps = {}, {}, {}

    def form(h):
        loads[h].wait()
        pulses = raw[:, :, columns_of(h)].reshape(-1, p.width)
        product = dot(weight[...], pulses)
        part[:, :, :, :, columns_of(h)] = product.astype(BF16).reshape(
            p.groups, p.comp, p.beam, p.rows, p.width
        )

    def start_one(g, h):
        one[g, h] = []
        for d in range(1, p.comp):
            peer = lax.rem(c + d, p.comp)
            k = (g * PIECES + h) * (p.comp - 1) + d - 1
            copy = remote(
                part.at[g, peer, :, :, columns_of(h)],
                recv_one.at[d - 1, g, :, :, columns_of(h)],
                one_send.at[k], one_recv.at[k], at(0, 0, d),
            )
            copy.start()
            one[g, h].append(copy)

    def start_two(g, h):
        for copy in one[g, h]:
            copy.wait_recv()
        total = part[g, c, :, :, columns_of(h)].astype(F32)
        for d in range(1, p.comp):
            total += recv_one[d - 1, g, :, :, columns_of(h)].astype(F32)
        held[g, :, :, columns_of(h)] = total.astype(BF16)
        two[g, h] = []
        for d in range(1, p.beam):
            peer = lax.rem(b + d, p.beam)
            k = (g * PIECES + h) * (p.beam - 1) + d - 1
            copy = remote(
                held.at[g, peer, :, columns_of(h)],
                recv_two.at[d - 1, g, :, columns_of(h)],
                two_send.at[k], two_recv.at[k], at(0, d, 0),
            )
            copy.start()
            two[g, h].append(copy)

    def finish(g, h):
        for copy in two[g, h]:
            copy.wait_recv()
        total = part[g, c, b, :, columns_of(h)].astype(F32)
        for d in range(1, p.comp):
            total += recv_one[d - 1, g, b, :, columns_of(h)].astype(F32)
        for d in range(1, p.beam):
            total += recv_two[d - 1, g, :, columns_of(h)].astype(F32)
        for a in range(p.width // radix):
            swap[pl.ds(h * (p.width // radix) + a, p.rows, stride=radix), :] = total[
                :, a * radix : (a + 1) * radix
            ]

    def compress(g):
        factor = p.length ** (-0.5)
        h_real = filt[pl.ds(0, radix, stride=2), :] * factor
        h_imag = filt[pl.ds(1, radix, stride=2), :] * factor
        span = p.group * radix

        @pl.loop(0, p.group // 2)
        def _(pair):
            sides = []
            for u in range(2):
                row = pl.multiple_of((2 * pair + u) * radix, radix)
                sides.append(
                    jnp.concatenate(
                        [swap[pl.ds(row, radix), :], swap[pl.ds(row + span, radix), :]], axis=0
                    )
                )
            high, low = split(jnp.concatenate(sides, axis=1))
            section = dot(first[...], high) + dot(first[...], low)
            cos_turn, sin_turn = turn[0], turn[1]
            turned = []
            for u in range(2):
                real = section[:radix, u * radix : (u + 1) * radix]
                imag = section[radix:, u * radix : (u + 1) * radix]
                turned.append(
                    jnp.concatenate(
                        [
                            real * cos_turn - imag * sin_turn,
                            real * sin_turn + imag * cos_turn,
                        ],
                        axis=1,
                    )
                )
            high, low = split(jnp.concatenate(turned, axis=0))
            both_last = (((1,), (1,)), ((), ()))
            spectrum = lax.dot_general(second[...], high, both_last, preferred_element_type=F32)
            spectrum += lax.dot_general(second[...], low, both_last, preferred_element_type=F32)
            for u in range(2):
                real = spectrum[:radix, u * radix : (u + 1) * radix]
                imag = spectrum[radix:, u * radix : (u + 1) * radix]
                row = 2 * pair + u
                blend[pl.ds(row, radix, stride=p.rows), :] = real * h_real - imag * h_imag
                blend[pl.ds(row + p.group, radix, stride=p.rows), :] = (
                    real * h_imag + imag * h_real
                )

        image[g] = blend[...].reshape(radix, p.rows, radix).astype(BF16)
        swaps[g] = []
        for i, (ds, dc) in enumerate(p.swap_peers):
            where = at(ds, 0, dc)
            begin = (where["sub"] * p.comp + where["comp"]) * p.share
            k = g * len(p.swap_peers) + i
            copy = remote(
                image.at[g, pl.ds(begin, p.share)],
                window.at[s, 1 + c, g],
                swap_send.at[k], swap_recv.at[k], where,
            )
            copy.start()
            swaps[g].append(copy)
        window[s, 1 + c, g] = image[g, pl.ds((s * p.comp + c) * p.share, p.share)]

    def halo_copy(g, step):
        near, far = (1, p.comp + 1) if step < 0 else (p.comp, 0)
        k = 2 * g + (0 if step < 0 else 1)
        return remote(
            window.at[:, near, g], window.at[:, far, g], halo_send.at[k], halo_recv.at[k],
            {"beam": b + step},
        )

    def start_halo(g):
        for copy in swaps[g]:
            copy.wait_recv()

        @pl.when(has_low)
        def _():
            halo_copy(g, -1).start()

        @pl.when(has_high)
        def _():
            halo_copy(g, 1).start()

    def wait_halo(g):
        @pl.when(has_low)
        def _():
            halo_copy(g, 1).wait_recv()
            halo_copy(g, -1).wait_send()

        @pl.when(has_high)
        def _():
            halo_copy(g, -1).wait_recv()
            halo_copy(g, 1).wait_send()

    def read_tables():
        tables[1, c] = table_ref[...]
        for copy in table_copies:
            copy.wait_recv()
        for j in range(p.padded // 128):
            block = tables[:, :, :, j * 128 : (j + 1) * 128].reshape(-1, 128)
            short = 128 - block.shape[0]
            if short > 0:
                block = jnp.concatenate([block, jnp.zeros((short, 128), F32)], axis=0)
            fields[j * 128 : (j + 1) * 128, :] = block.T
        zeros = jnp.zeros(window.shape[:1] + window.shape[2:], BF16)

        @pl.when(jnp.logical_not(has_low))
        def _():
            window[:, 0] = zeros

        @pl.when(jnp.logical_not(has_high))
        def _():
            window[:, p.comp + 1] = zeros

    def fields_of(level, side):
        for step, begin, size in p.pieces(level):
            row = side * p.columns + p.first * (2 ** (level + 1) - 2) + begin
            device = (step + p.comp) if 0 <= step < p.comp else (p.comp - 1 if step < 0 else 2 * p.comp)
            yield step, size, row, device * FIELDS

    def build(level):
        depth, size = p.depths[level], p.sizes[level]
        child = p.first * 2**level
        lane = lax.broadcasted_iota(jnp.int32, (1, depth), 1)
        if level == 0:
            within, upper = bits(lane, p.group)
            half, upper = bits(upper, 2)
            group_at, slot = bits(upper, p.groups)
            beam_at = slot * p.first + group_at * p.group + within
        else:
            half = jnp.where(lane < depth // 2, 0, 1)
            beam_at = lane - half * (depth // 2)
        begin = p.first if level == 0 else EXTRA
        for side in range(2):
            done = 0
            for step, rows, row, base in fields_of(level, side):
                block = fields[row : row + rows, base : base + FIELDS]
                shift = block[:, BAND : BAND + 1].astype(jnp.int32)
                tap = beam_at - begin - step * child - shift
                band = jnp.zeros((rows, depth), F32)
                for t in range(BAND):
                    band += jnp.where(tap == t, block[:, t : t + 1], 0.0)
                if step < 0:
                    band = jnp.where(has_low, band, 0.0)
                if step >= p.comp:
                    band = jnp.where(has_high, band, 0.0)
                for r in range(2):
                    high, low = split(jnp.where(half == r, band, 0.0))
                    lhs[level][side, 0, r * size + done : r * size + done + rows, :] = high
                    lhs[level][side, 1, r * size + done : r * size + done + rows, :] = low
                delay[level][side, done : done + rows, :] = jnp.broadcast_to(
                    block[:, BAND + 1 : BAND + 2], (rows, radix)
                )
                done += rows

    def build_phases(begin, end):
        start = (s * p.comp + c) * p.share

        @pl.loop(begin, end)
        def _(m):
            for level in range(levels):
                for side in range(2):
                    factor = delay[level][side]
                    lane = lax.broadcasted_iota(jnp.int32, factor.shape, 1)
                    place = ((start + m) * radix + lane).astype(F32)
                    phase_angle = factor * (1.0 + place / p.length)
                    phase[level][0, side, m] = jnp.cos(phase_angle)
                    phase[level][1, side, m] = jnp.sin(phase_angle)

    def merge(m):
        def pair(load):
            return jnp.concatenate([load(m), load(m + 1)], axis=1)

        images = [
            pair(lambda k, i=i: window[i, :, :, k].reshape(p.depths[0], radix))
            for i in range(p.sub)
        ]
        for level in range(levels):
            size = p.sizes[level]
            merged = []
            for g in range(len(images) // 2):
                real, imag = 0.0, 0.0
                for side in range(2):
                    child = images[2 * g + side]
                    mixed = dot(lhs[level][side, 0], child) + dot(lhs[level][side, 1], child)
                    cosine = pair(lambda k: phase[level][0, side, k])
                    sine = pair(lambda k: phase[level][1, side, k])
                    real += cosine * mixed[:size] - sine * mixed[size:]
                    imag += sine * mixed[:size] + cosine * mixed[size:]
                merged.append((real, imag))
            if level + 1 < levels:
                images = [jnp.concatenate(parts, axis=0).astype(BF16) for parts in merged]
        for r in range(2):
            for k in range(p.comp):
                for u in range(2):
                    value = merged[0][r][k * p.outs : (k + 1) * p.outs, u * radix : (u + 1) * radix]
                    final[k, m + u, r * p.outs : (r + 1) * p.outs, :] = value
                    outbound[k, m + u, r * p.outs : (r + 1) * p.outs, :] = value.astype(BF16)

    def place_out(source, m, column):
        for r in range(2):
            value = source[r * p.outs : (r + 1) * p.outs].astype(F32)
            out_ref[pl.ds(2 * (column * p.share + m) + r, p.outs, stride=2 * p.quarter), :] = value

    units = [(g, h) for g in range(p.groups) for h in range(PIECES)]
    total_units = len(units)
    per_step = -(-p.share // PIECES)
    pending = []
    for u in range(total_units + LAG + LAG_TWO):
        if u < PIECES:
            form(u)
        if u < total_units:
            start_one(*units[u])
        if 0 <= u - LAG < total_units:
            start_two(*units[u - LAG])
        v = u - LAG - LAG_TWO
        if pending and v >= pending[0][0]:
            start_halo(pending.pop(0)[1])
        if u == PIECES:
            read_tables()
            for copy in constants:
                copy.wait()
            for level in range(levels):
                build(level)
        if PIECES <= u < 2 * PIECES:
            begin = min((u - PIECES) * per_step, p.share)
            end = min(begin + per_step, p.share)
            if end > begin:
                build_phases(begin, end)
        if v >= 0:
            finish(*units[v])
            g, h = units[v]
            if h == PIECES - 1:
                compress(g)
                pending.append((v + 2, g))
    for _, g in pending:
        start_halo(g)
    for g in range(p.groups):
        wait_halo(g)

    chunk = p.share // OUT_PIECES
    outs = []
    for o in range(OUT_PIECES):
        @pl.loop(0, chunk // 2)
        def _(i, o=o):
            merge(o * chunk + 2 * i)

        for d in range(1, p.comp):
            peer = lax.rem(c + d, p.comp)
            k = (d - 1) * OUT_PIECES + o
            copy = remote(
                outbound.at[peer, pl.ds(o * chunk, chunk)],
                inbound.at[d - 1, pl.ds(o * chunk, chunk)],
                out_send.at[k], out_recv.at[k], at(0, 0, d),
            )
            copy.start()
            outs.append((o, d, copy))

    @pl.loop(0, p.share)
    def _(m):
        place_out(final[c, m], m, c)

    for o, d, copy in outs:
        copy.wait_recv()
        origin = lax.rem(c + p.comp - d, p.comp)

        @pl.loop(0, chunk)
        def _(i, o=o, d=d, origin=origin):
            place_out(inbound[d - 1, o * chunk + i], o * chunk + i, origin)

    for copy in itertools.chain(
        table_copies, *one.values(), *two.values(), *swaps.values(), (entry[2] for entry in outs)
    ):
        copy.wait_send()


def fused(plan, angle, raw, filt, table):
    p = plan
    constants = real_form(p.radix)
    any_space = pl.BlockSpec(memory_space=pl.ANY)
    vmem = pl.BlockSpec(memory_space=pltpu.VMEM)
    dma = pltpu.SemaphoreType.DMA
    radix = p.radix
    units = p.groups * PIECES
    return pl.pallas_call(
        functools.partial(fused_kernel, p),
        out_shape=jax.ShapeDtypeStruct((p.outs * 2 * p.quarter, radix), F32),
        in_specs=[vmem, any_space, any_space, vmem, any_space, any_space, any_space],
        out_specs=vmem,
        scratch_shapes=[
            pltpu.VMEM(raw.shape, BF16),
            pltpu.VMEM((2 * p.beams, 2 * p.pulses), BF16),
            pltpu.VMEM((p.groups, p.comp, p.beam, p.rows, p.length), BF16),
            pltpu.VMEM((p.comp - 1, p.groups, p.beam, p.rows, p.length), BF16),
            pltpu.VMEM((p.groups, p.beam, p.rows, p.length), BF16),
            pltpu.VMEM((p.beam - 1, p.groups, p.rows, p.length), BF16),
            pltpu.VMEM((p.rows * radix, radix), F32),
            pltpu.VMEM((2 * radix, 2 * radix), BF16),
            pltpu.VMEM((2 * radix, 2 * radix), BF16),
            pltpu.VMEM((2, radix, radix), F32),
            pltpu.VMEM((2 * radix, radix), F32),
            pltpu.VMEM((p.rows * radix, radix), F32),
            pltpu.VMEM((p.groups, radix, p.rows, radix), BF16),
            pltpu.VMEM((p.sub, p.slots, p.groups, p.share, p.rows, radix), BF16),
            pltpu.VMEM((3, p.comp, FIELDS, p.padded), F32),
            pltpu.VMEM((p.padded, 128), F32),
            *[pltpu.VMEM((2, 2, 2 * n, k), BF16) for n, k in zip(p.sizes, p.depths)],
            *[pltpu.VMEM((2, n, radix), F32) for n in p.sizes],
            *[pltpu.VMEM((2, 2, p.share, n, radix), F32) for n in p.sizes],
            pltpu.VMEM((p.comp, p.share, 2 * p.outs, radix), F32),
            pltpu.VMEM((p.comp, p.share, 2 * p.outs, radix), BF16),
            pltpu.VMEM((p.comp - 1, p.share, 2 * p.outs, radix), BF16),
            dma((PIECES,)),
            dma((4,)),
            dma((len(p.table_peers),)),
            dma((len(p.table_peers),)),
            dma((units * (p.comp - 1),)),
            dma((units * (p.comp - 1),)),
            dma((units * (p.beam - 1),)),
            dma((units * (p.beam - 1),)),
            dma((p.groups * len(p.swap_peers),)),
            dma((p.groups * len(p.swap_peers),)),
            dma((2 * p.groups,)),
            dma((2 * p.groups,)),
            dma(((p.comp - 1) * OUT_PIECES,)),
            dma(((p.comp - 1) * OUT_PIECES,)),
        ],
        compiler_params=pltpu.CompilerParams(
            collective_id=0, has_side_effects=True, vmem_limit_bytes=58 * 2**20
        ),
    )(
        angle, raw, filt, table, jnp.asarray(constants.T), jnp.asarray(constants.T),
        jnp.asarray(twiddle(radix)),
    )


def body(raw_pulses, range_filter, steer_angle, band_offsets, band_weights, beam_delay):
    counts = (lax.axis_size("sub"), lax.axis_size("beam"), lax.axis_size("comp"))
    columns = band_offsets.shape[1]
    plan = Plan(counts, steer_angle.shape, raw_pulses.shape[2], columns)
    radix = plan.radix
    table = jnp.concatenate(
        [
            band_weights.transpose(2, 0, 1).reshape(BAND, 2 * columns),
            band_offsets.astype(F32).reshape(1, 2 * columns),
            beam_delay.reshape(1, 2 * columns),
        ],
        axis=0,
    )
    table = jnp.pad(
        table, ((0, FIELDS - table.shape[0]), (0, plan.padded - 2 * columns))
    )
    filt = range_filter.reshape(2, radix, radix).transpose(1, 0, 2).reshape(2 * radix, radix)
    out = fused(plan, steer_angle, raw_pulses, filt, table)
    out = out.reshape(plan.outs, plan.quarter, 2, radix).transpose(0, 2, 1, 3)
    return out.reshape(plan.outs, 2, plan.quarter * radix)


def solution(mesh):
    in_specs = (
        P(("sub", "beam", "comp"), None, None),
        P(),
        P(None, ("sub", "beam", "comp")),
        P(None, ("beam", "comp")),
        P(None, ("beam", "comp"), None),
        P(None, ("beam", "comp")),
    )
    out_specs = P(("beam", "comp"), None, "sub")
    return jax.shard_map(body, mesh=mesh, in_specs=in_specs, out_specs=out_specs, check_vma=False)
```

time: 110 us -> 92.1 us (0.84); the launches traced: 108 us -> 91.8 us
  other arithmetic: 12 us -> 1.29 us
  local copies, waits for them, and re-layouts: 8.49 us -> 3.93 us
  matrix products: 4.19 us -> 0 us
  Pallas kernels: 83.2 us -> 86.6 us
    dot_general x7 -> x0, matrix products: 4.19 us -> none  [the longest x4 2.17 us: merge(): jnp.einsum('jw,gpwr->gpjr', both, paired[:, c], preferred_element_type=jn...]
    add x10 -> x0, other arithmetic: 4.07 us -> none  [the longest x4 2.4 us: merge(): blended = blended[:, :, :count] + blended[:, :, count:]]
    another operation x10 -> x0, other arithmetic: 3.39 us -> none  [the longest x1 0.9 us: steering(): jnp.stack([imag_part, real_part], -1).reshape(phase_angle.shape[0], -1)]
    pallas_call x3 -> x1, Pallas kernels: 83.2 us -> 86.6 us  [fused(): pl.pallas_call(functools.partial(fused_kernel, p), out_shape=jax.ShapeDty...]
    another operation x4 -> x0, local copies, waits for them, and re-layouts: 2.31 us -> none  [the longest x1 1.78 us: body(): return jnp.stack([real[0], imag[0]], 1)]
    sub x2 -> x0, other arithmetic: 2 us -> none  [the longest x1 1.86 us: phases(): cosine = cos_one * cos_two - sin_one * sin_two]
    broadcast_in_dim x4 -> x0, local copies, waits for them, and re-layouts: 1.63 us -> none  [band_matrix(): jnp.where(matches, weight[:, :, None], jnp.zeros_like(weight)[:, :, None])]
    add x1 -> x0, local copies, waits for them, and re-layouts: 1.56 us -> none  [phases(): sine = sin_one * cos_two + cos_one * sin_two]
where the time goes in v1:
time: 92.1 us; the launch traced here: 91.8 us
  Pallas kernels  86.6 us (94%)
  local copies, waits for them, and re-layouts  3.93 us (4%)
  other arithmetic  1.29 us (1%)
    pallas_call x1, Pallas kernels, fused(): pl.pallas_call(functools.partial(fused_kernel, p), out_shape=jax.ShapeDty...  86.6 us
    unnamed x1, local copies, waits for them, and re-layouts  2.31 us

profile of v1, /device:TPU:0, one launch (start us, length us, event | category | flops | bytes accessed | tf_op | source)
XLA Modules:
  0.0 91.8 jit_solution(16024302188932037922)
XLA Ops:
  0.0 0.8 reshape.25
  0.8 0.7 convert_element_type.5
  1.4 0.1 reshape.24
  1.5 0.7 copy.11
  2.2 0.1 reshape.23
  2.3 0.6 select_maximum_fusion.table_ref
  2.9 86.6 %shard_map.91 = f32[2048,128]{1,0:T(8,128)} custom-call(f32[64,128]{1,0:T(8,128)} %angle_ref.1, bf16[128,2,16384]{2,1,0:T(2,128)(2,1)} %raw_hbm.1, f32[256,128]{1,0:T(8,128)} %bitcast.12, f32[16,128]{1,0:T(8,128)} %select_maximum_fusion.table_ref, bf16[256,256]{1,0:T(8,128)(2,1)} %constant.7.clone.first_hbm.second_hbm, ...), custom_call_target="tpu_custom_call" | custom-call | tf_op jit(solution)/shard_map/pallas_call | solution.py:546
  89.5 2.3 %copy.14 = f32[32,2,4096]{2,1,0:T(2,128)} copy(f32[32,2,4096]{2,1,0:T(2,128)} %bitcast.11) | data formatting | bytes 2097152

commit v2 on v1

--- a/solution.py
+++ b/solution.py
@@ -12,12 +12,15 @@
 
 BAND = 8
 EXTRA = 8
-FIELDS = 16
-GROUP = 4
+SIDE = 12
+GROUP = 2
 PIECES = 8
-LAG = 3
-LAG_TWO = 2
+LAG = 4
+LAG_TWO = 3
 OUT_PIECES = 4
+HALO_LAG = 4
+LIMIT = 54 * 2**20
+STORES = 4
 MESH = pl.DeviceIdType.MESH
 F32 = jnp.float32
 BF16 = jnp.bfloat16
@@ -70,7 +73,8 @@
         self.quarter = self.radix // self.sub
         self.share = self.quarter // self.comp
         self.outs = self.first * self.sub
-        self.padded = -(-2 * columns // 128) * 128
+        self.padded = -(-columns // 128) * 128
+        self.stages = self.beam.bit_length() - 1
         self.slots = self.comp + 2
         self.factor = float(self.pulses * self.blocks) ** (-0.5)
         self.sizes = []
@@ -82,12 +86,11 @@
         near |= {(d, 0, e) for d in range(self.sub) for e in range(self.comp)}
         near |= {(0, d, 0) for d in range(self.beam)}
         self.peers = sorted({(d % self.sub, e % self.beam, f % self.comp) for d, e, f in near} - {(0, 0, 0)})
-        self.table_peers = [
-            (d, e)
-            for d in (-1, 0, 1)
-            for e in range(self.comp)
-            if (d % self.beam, e) != (0, 0)
-        ]
+        need = BAND // 2
+        for _ in range(self.levels - 1):
+            need = (need + 1) // 2 + BAND // 2
+        need = min(need, self.first) if self.comp > 1 else self.first
+        self.edges = [g for g in range(self.groups) if g * self.group < need]
         self.swap_peers = [
             (d, e) for d in range(self.sub) for e in range(self.comp) if (d, e) != (0, 0)
         ]
@@ -101,19 +104,23 @@
 
 
 def fused_kernel(
-    plan, angle_ref, raw_hbm, filter_hbm, table_ref, first_hbm, second_hbm, turn_hbm, out_ref,
-    raw, weight, part, recv_one, held, recv_two, swap, first, second, turn, filt, blend, image,
-    window, tables, fields, *rest,
+    plan, angle_hbm, raw_hbm, filter_hbm, weights_hbm, offsets_hbm, delay_hbm, first_hbm,
+    second_hbm, turn_hbm, out_ref, angle_ref, weights_ref, offsets_ref, delay_ref, raw, weight, part, recv_one, swap, first, second, turn, filt,
+    blend, image, window, mine, tables, fields, *rest,
 ):
     p = plan
     levels = p.levels
-    lhs = rest[:levels]
-    delay = rest[levels : 2 * levels]
-    phase = rest[2 * levels : 3 * levels]
+    rest = list(rest)
+
+    def take(number):
+        taken = rest[:number]
+        del rest[:number]
+        return taken
+
+    held, recv_two = take(p.stages), take(p.stages)
+    lhs, delay, phase = take(levels), take(levels), take(levels)
     (final, outbound, inbound, load_sem, const_sem, table_send, table_recv, one_send, one_recv,
-     two_send, two_recv, swap_send, swap_recv, halo_send, halo_recv, out_send, out_recv) = rest[
-        3 * levels :
-    ]
+     two_send, two_recv, swap_send, swap_recv, halo_send, halo_recv, out_send, out_recv) = rest
     s = lax.axis_index("sub")
     b = lax.axis_index("beam")
     c = lax.axis_index("comp")
@@ -134,6 +141,8 @@
             device_id_type=MESH,
         )
 
+    angle_load = pltpu.make_async_copy(angle_hbm, angle_ref, const_sem.at[7])
+    angle_load.start()
     loads = []
     for h in range(PIECES):
         cols = pl.ds(h * p.width, p.width)
@@ -144,16 +153,22 @@
     constants = [
         pltpu.make_async_copy(source, target, const_sem.at[i])
         for i, (source, target) in enumerate(
-            [(first_hbm, first), (second_hbm, second), (turn_hbm, turn), (filter_hbm, filt)]
+            [
+                (weights_hbm, weights_ref), (offsets_hbm, offsets_ref), (delay_hbm, delay_ref),
+                (first_hbm, first), (second_hbm, second), (turn_hbm, turn), (filter_hbm, filt),
+            ]
         )
     ]
     for copy in constants:
         copy.start()
 
+    window[:, 0] = jnp.zeros(window.shape[:1] + window.shape[2:], BF16)
+    window[:, p.comp + 1] = jnp.zeros(window.shape[:1] + window.shape[2:], BF16)
     barrier = pltpu.get_barrier_semaphore()
     for place in p.peers:
         pl.semaphore_signal(barrier, inc=1, device_id=at(*place), device_id_type=MESH)
 
+    angle_load.wait()
     angle = angle_ref[...]
     cos_part = (jnp.cos(angle) * p.factor).astype(BF16)
     sin_part = (jnp.sin(angle) * p.factor).astype(BF16)
@@ -177,10 +192,14 @@
             value, jnp.full_like(value, size.bit_length() - 1)
         )
 
+    def order_of(group_at, comp_at):
+        return jnp.where(comp_at == p.comp - 1, p.groups - 1 - group_at, group_at)
+
     within, upper = bits(target, p.group)
     half, upper = bits(upper, 2)
     beam_at, upper = bits(upper, p.beam)
     comp_at, group_at = bits(upper, p.comp)
+    group_at = order_of(group_at, comp_at)
     origin = half * p.beams + (
         (beam_at * p.comp + comp_at) * p.first + group_at * p.group + within
     )
@@ -189,25 +208,44 @@
 
     pl.semaphore_wait(barrier, len(p.peers))
 
-    started = []
-    table_copies = []
-
-    def table_copy(i, db, dc):
-        return remote(
-            table_ref,
-            tables.at[1 - db, lax.rem(c + p.comp, p.comp)],
-            table_send.at[i], table_recv.at[i], at(0, db, dc),
-        )
-
-    for i, (db, dc) in enumerate(p.table_peers):
-        copy = table_copy(i, db, dc)
-        copy.start()
-        table_copies.append(copy)
+    for copy in constants[:3]:
+        copy.wait()
+    mine[...] = jnp.zeros(mine.shape, F32)
+    for side in range(2):
+        row = side * SIDE
+        mine[row : row + BAND, : p.columns] = weights_ref[side]
+        mine[row + BAND : row + BAND + 1, : p.columns] = offsets_ref[side : side + 1].astype(F32)
+        mine[row + BAND + 1 : row + BAND + 2, : p.columns] = delay_ref[side : side + 1]
+    tables[1 + c] = mine[...]
+
+    def table_copy(db, dc):
+        slot = 1 + c if db == 0 else (0 if db > 0 else p.comp + 1)
+        k = (db + 1) * p.comp + dc
+        r = dc if db == 0 else (0 if db > 0 else p.comp)
+        return remote(mine, tables.at[slot], table_send.at[k], table_recv.at[r], at(0, db, dc))
+
+    def table_ends(action):
+        @pl.when(c == p.comp - 1)
+        def _():
+            for e in range(p.comp):
+                action(table_copy(1, e))
+
+        @pl.when(c == 0)
+        def _():
+            for e in range(p.comp):
+                action(table_copy(-1, e))
+
+    for e in range(1, p.comp):
+        table_copy(0, e).start()
+    table_ends(lambda copy: copy.start())
 
     def columns_of(h):
         return pl.ds(h * p.width, p.width)
 
     one, two, swaps = {}, {}, {}
+
+    def bit(stage):
+        return lax.rem(lax.div(b, 2**stage), 2)
 
     def form(h):
         loads[h].wait()
@@ -230,39 +268,43 @@
             copy.start()
             one[g, h].append(copy)
 
+    def send_two(stage, g, h, total):
+        held[stage][g, :, :, :, columns_of(h)] = total.astype(BF16).reshape(
+            -1, 2, p.rows, p.width
+        )
+        k = (g * PIECES + h) * p.stages + stage
+        copy = remote(
+            held[stage].at[g, :, 1 - bit(stage), :, columns_of(h)],
+            recv_two[stage].at[g, :, :, columns_of(h)],
+            two_send.at[k], two_recv.at[k],
+            {"beam": b + (1 - 2 * bit(stage)) * 2**stage},
+        )
+        copy.start()
+        two[stage, g, h] = copy
+
     def start_two(g, h):
         for copy in one[g, h]:
             copy.wait_recv()
         total = part[g, c, :, :, columns_of(h)].astype(F32)
         for d in range(1, p.comp):
             total += recv_one[d - 1, g, :, :, columns_of(h)].astype(F32)
-        held[g, :, :, columns_of(h)] = total.astype(BF16)
-        two[g, h] = []
-        for d in range(1, p.beam):
-            peer = lax.rem(b + d, p.beam)
-            k = (g * PIECES + h) * (p.beam - 1) + d - 1
-            copy = remote(
-                held.at[g, peer, :, columns_of(h)],
-                recv_two.at[d - 1, g, :, columns_of(h)],
-                two_send.at[k], two_recv.at[k], at(0, d, 0),
-            )
-            copy.start()
-            two[g, h].append(copy)
+        send_two(0, g, h, total)
+
+    def gathered(stage, g, h):
+        two[stage, g, h].wait_recv()
+        total = held[stage][g, :, bit(stage), :, columns_of(h)].astype(F32)
+        return total + recv_two[stage][g, :, :, columns_of(h)].astype(F32)
 
     def finish(g, h):
-        for copy in two[g, h]:
-            copy.wait_recv()
-        total = part[g, c, b, :, columns_of(h)].astype(F32)
-        for d in range(1, p.comp):
-            total += recv_one[d - 1, g, b, :, columns_of(h)].astype(F32)
-        for d in range(1, p.beam):
-            total += recv_two[d - 1, g, :, columns_of(h)].astype(F32)
+        total = gathered(p.stages - 1, g, h)[0]
         for a in range(p.width // radix):
             swap[pl.ds(h * (p.width // radix) + a, p.rows, stride=radix), :] = total[
                 :, a * radix : (a + 1) * radix
             ]
 
-    def compress(g):
+    deferred = []
+
+    def compress(g, deferring):
         factor = p.length ** (-0.5)
         h_real = filt[pl.ds(0, radix, stride=2), :] * factor
         h_imag = filt[pl.ds(1, radix, stride=2), :] * factor
@@ -308,76 +350,80 @@
                 )
 
         image[g] = blend[...].reshape(radix, p.rows, radix).astype(BF16)
-        swaps[g] = []
-        for i, (ds, dc) in enumerate(p.swap_peers):
-            where = at(ds, 0, dc)
-            begin = (where["sub"] * p.comp + where["comp"]) * p.share
-            k = g * len(p.swap_peers) + i
-            copy = remote(
-                image.at[g, pl.ds(begin, p.share)],
-                window.at[s, 1 + c, g],
-                swap_send.at[k], swap_recv.at[k], where,
-            )
-            copy.start()
-            swaps[g].append(copy)
         window[s, 1 + c, g] = image[g, pl.ds((s * p.comp + c) * p.share, p.share)]
-
-    def halo_copy(g, step):
+        number = OUT_PIECES if g == p.groups - 1 else 1
+        size = p.share // number
+        for o in range(number):
+            swaps[g, o] = []
+            for i, (ds, dc) in enumerate(p.swap_peers):
+                where = at(ds, 0, dc)
+                begin = (where["sub"] * p.comp + where["comp"]) * p.share + o * size
+                k = (g + o) * len(p.swap_peers) + i
+                copy = remote(
+                    image.at[g, pl.ds(begin, size)],
+                    window.at[s, 1 + c, g, pl.ds(o * size, size)],
+                    swap_send.at[k], swap_recv.at[k], where,
+                )
+                swaps[g, o].append(copy)
+                if dc == 0 or not deferring:
+                    copy.start()
+                else:
+                    deferred.append(copy)
+
+    def halo_copy(g, o, step):
         near, far = (1, p.comp + 1) if step < 0 else (p.comp, 0)
-        k = 2 * g + (0 if step < 0 else 1)
+        size = p.share // (OUT_PIECES if g == p.groups - 1 else 1)
+        k = 2 * (g + o) + (0 if step < 0 else 1)
         return remote(
-            window.at[:, near, g], window.at[:, far, g], halo_send.at[k], halo_recv.at[k],
-            {"beam": b + step},
-        )
-
-    def start_halo(g):
-        for copy in swaps[g]:
+            window.at[:, near, g, pl.ds(o * size, size)],
+            window.at[:, far, g, pl.ds(o * size, size)],
+            halo_send.at[k], halo_recv.at[k], {"beam": b + step},
+        )
+
+    def start_halo(g, o=0):
+        for copy in swaps[g, o]:
             copy.wait_recv()
+        if g not in p.edges:
+            return
 
         @pl.when(has_low)
         def _():
-            halo_copy(g, -1).start()
+            halo_copy(g, o, -1).start()
 
         @pl.when(has_high)
         def _():
-            halo_copy(g, 1).start()
-
-    def wait_halo(g):
+            halo_copy(g, o, 1).start()
+
+    def wait_halo(g, o=0):
+        if g not in p.edges:
+            return
+
         @pl.when(has_low)
         def _():
-            halo_copy(g, 1).wait_recv()
-            halo_copy(g, -1).wait_send()
+            halo_copy(g, o, 1).wait_recv()
+            halo_copy(g, o, -1).wait_send()
 
         @pl.when(has_high)
         def _():
-            halo_copy(g, -1).wait_recv()
-            halo_copy(g, 1).wait_send()
+            halo_copy(g, o, -1).wait_recv()
+            halo_copy(g, o, 1).wait_send()
 
     def read_tables():
-        tables[1, c] = table_ref[...]
-        for copy in table_copies:
-            copy.wait_recv()
+        for e in range(1, p.comp):
+            table_copy(0, e).wait_recv()
+        table_copy(1, 0).wait_recv()
+        table_copy(-1, 0).wait_recv()
         for j in range(p.padded // 128):
-            block = tables[:, :, :, j * 128 : (j + 1) * 128].reshape(-1, 128)
+            block = tables[:, :, j * 128 : (j + 1) * 128].reshape(-1, 128)
             short = 128 - block.shape[0]
             if short > 0:
                 block = jnp.concatenate([block, jnp.zeros((short, 128), F32)], axis=0)
             fields[j * 128 : (j + 1) * 128, :] = block.T
-        zeros = jnp.zeros(window.shape[:1] + window.shape[2:], BF16)
-
-        @pl.when(jnp.logical_not(has_low))
-        def _():
-            window[:, 0] = zeros
-
-        @pl.when(jnp.logical_not(has_high))
-        def _():
-            window[:, p.comp + 1] = zeros
 
     def fields_of(level, side):
         for step, begin, size in p.pieces(level):
-            row = side * p.columns + p.first * (2 ** (level + 1) - 2) + begin
-            device = (step + p.comp) if 0 <= step < p.comp else (p.comp - 1 if step < 0 else 2 * p.comp)
-            yield step, size, row, device * FIELDS
+            row = p.first * (2 ** (level + 1) - 2) + begin
+            yield step, size, row, (step + 1) * 2 * SIDE + side * SIDE
 
     def build(level):
         depth, size = p.depths[level], p.sizes[level]
@@ -387,6 +433,8 @@
             within, upper = bits(lane, p.group)
             half, upper = bits(upper, 2)
             group_at, slot = bits(upper, p.groups)
+            comp_at = jnp.where(slot == 0, p.comp - 1, jnp.where(slot > p.comp, 0, slot - 1))
+            group_at = order_of(group_at, comp_at)
             beam_at = slot * p.first + group_at * p.group + within
         else:
             half = jnp.where(lane < depth // 2, 0, 1)
@@ -395,7 +443,7 @@
         for side in range(2):
             done = 0
             for step, rows, row, base in fields_of(level, side):
-                block = fields[row : row + rows, base : base + FIELDS]
+                block = fields[row : row + rows, base : base + SIDE]
                 shift = block[:, BAND : BAND + 1].astype(jnp.int32)
                 tap = beam_at - begin - step * child - shift
                 band = jnp.zeros((rows, depth), F32)
@@ -465,25 +513,35 @@
 
     units = [(g, h) for g in range(p.groups) for h in range(PIECES)]
     total_units = len(units)
-    per_step = -(-p.share // PIECES)
+    idle = range(PIECES, 2 * PIECES)
+    per_step = -(-p.share // len(idle))
     pending = []
-    for u in range(total_units + LAG + LAG_TWO):
+    last = p.groups - 1
+    drain = LAG + LAG_TWO * p.stages
+    for u in range(total_units + drain):
         if u < PIECES:
             form(u)
         if u < total_units:
             start_one(*units[u])
+        if u == total_units - 1:
+            for copy in deferred:
+                copy.start()
         if 0 <= u - LAG < total_units:
             start_two(*units[u - LAG])
-        v = u - LAG - LAG_TWO
-        if pending and v >= pending[0][0]:
+        for stage in range(1, p.stages):
+            v = u - LAG - LAG_TWO * stage
+            if 0 <= v < total_units:
+                send_two(stage, *units[v], gathered(stage - 1, *units[v]))
+        v = u - drain
+        while pending and v >= pending[0][0]:
             start_halo(pending.pop(0)[1])
         if u == PIECES:
             read_tables()
-            for copy in constants:
+            for copy in constants[3:]:
                 copy.wait()
             for level in range(levels):
                 build(level)
-        if PIECES <= u < 2 * PIECES:
+        if u in idle:
             begin = min((u - PIECES) * per_step, p.share)
             end = min(begin + per_step, p.share)
             if end > begin:
@@ -492,18 +550,20 @@
             finish(*units[v])
             g, h = units[v]
             if h == PIECES - 1:
-                compress(g)
-                pending.append((v + 2, g))
+                compress(g, u < total_units)
+                if g < last:
+                    pending.append((max(v + HALO_LAG, total_units - drain + 4), g))
     for _, g in pending:
         start_halo(g)
-    for g in range(p.groups):
+    for g in range(last):
         wait_halo(g)
 
     chunk = p.share // OUT_PIECES
     outs = []
-    for o in range(OUT_PIECES):
+
+    def merge_piece(o):
         @pl.loop(0, chunk // 2)
-        def _(i, o=o):
+        def _(i):
             merge(o * chunk + 2 * i)
 
         for d in range(1, p.comp):
@@ -517,6 +577,15 @@
             copy.start()
             outs.append((o, d, copy))
 
+    for o in range(OUT_PIECES):
+        start_halo(last, o)
+        if last not in p.edges:
+            merge_piece(o)
+    if last in p.edges:
+        for o in range(OUT_PIECES):
+            wait_halo(last, o)
+            merge_piece(o)
+
     @pl.loop(0, p.share)
     def _(m):
         place_out(final[c, m], m, c)
@@ -529,32 +598,62 @@
         def _(i, o=o, d=d, origin=origin):
             place_out(inbound[d - 1, o * chunk + i], o * chunk + i, origin)
 
+    for e in range(1, p.comp):
+        table_copy(0, e).wait_send()
+    table_ends(lambda copy: copy.wait_send())
     for copy in itertools.chain(
-        table_copies, *one.values(), *two.values(), *swaps.values(), (entry[2] for entry in outs)
+        *one.values(), two.values(), *swaps.values(), (entry[2] for entry in outs)
     ):
         copy.wait_send()
 
 
-def fused(plan, angle, raw, filt, table):
+def store_kernel(value_ref, out_hbm, sem):
+    size = value_ref.shape[0] // STORES
+    copies = [
+        pltpu.make_async_copy(
+            value_ref.at[pl.ds(i * size, size)], out_hbm.at[pl.ds(i * size, size)], sem.at[i]
+        )
+        for i in range(STORES)
+    ]
+    for copy in copies:
+        copy.start()
+    for copy in copies:
+        copy.wait()
+
+
+def store(value):
+    return pl.pallas_call(
+        store_kernel,
+        out_shape=jax.ShapeDtypeStruct(value.shape, value.dtype),
+        in_specs=[pl.BlockSpec(memory_space=pltpu.VMEM)],
+        out_specs=pl.BlockSpec(memory_space=pl.ANY),
+        scratch_shapes=[pltpu.SemaphoreType.DMA((STORES,))],
+        compiler_params=pltpu.CompilerParams(vmem_limit_bytes=8 * 2**20),
+    )(value)
+
+
+def fused(plan, angle, raw, filt, weights, offsets, delay):
     p = plan
     constants = real_form(p.radix)
-    any_space = pl.BlockSpec(memory_space=pl.ANY)
-    vmem = pl.BlockSpec(memory_space=pltpu.VMEM)
     dma = pltpu.SemaphoreType.DMA
     radix = p.radix
     units = p.groups * PIECES
+    halves = [p.beam // 2 ** (t + 1) for t in range(p.stages)]
+    swap_count = p.groups - 1 + OUT_PIECES
     return pl.pallas_call(
         functools.partial(fused_kernel, p),
-        out_shape=jax.ShapeDtypeStruct((p.outs * 2 * p.quarter, radix), F32),
-        in_specs=[vmem, any_space, any_space, vmem, any_space, any_space, any_space],
-        out_specs=vmem,
+        out_shape=pltpu.VMEM((p.outs * 2 * p.quarter, radix), F32),
+        in_specs=[pl.BlockSpec(memory_space=pltpu.HBM)] * 9,
+        out_specs=pl.BlockSpec(memory_space=pltpu.VMEM),
         scratch_shapes=[
+            pltpu.VMEM(angle.shape, F32),
+            pltpu.VMEM(weights.shape, F32),
+            pltpu.VMEM(offsets.shape, jnp.int32),
+            pltpu.VMEM(delay.shape, F32),
             pltpu.VMEM(raw.shape, BF16),
             pltpu.VMEM((2 * p.beams, 2 * p.pulses), BF16),
             pltpu.VMEM((p.groups, p.comp, p.beam, p.rows, p.length), BF16),
             pltpu.VMEM((p.comp - 1, p.groups, p.beam, p.rows, p.length), BF16),
-            pltpu.VMEM((p.groups, p.beam, p.rows, p.length), BF16),
-            pltpu.VMEM((p.beam - 1, p.groups, p.rows, p.length), BF16),
             pltpu.VMEM((p.rows * radix, radix), F32),
             pltpu.VMEM((2 * radix, 2 * radix), BF16),
             pltpu.VMEM((2 * radix, 2 * radix), BF16),
@@ -563,8 +662,11 @@
             pltpu.VMEM((p.rows * radix, radix), F32),
             pltpu.VMEM((p.groups, radix, p.rows, radix), BF16),
             pltpu.VMEM((p.sub, p.slots, p.groups, p.share, p.rows, radix), BF16),
-            pltpu.VMEM((3, p.comp, FIELDS, p.padded), F32),
+            pltpu.VMEM((2 * SIDE, p.padded), F32),
+            pltpu.VMEM((p.slots, 2 * SIDE, p.padded), F32),
             pltpu.VMEM((p.padded, 128), F32),
+            *[pltpu.VMEM((p.groups, n, 2, p.rows, p.length), BF16) for n in halves],
+            *[pltpu.VMEM((p.groups, n, p.rows, p.length), BF16) for n in halves],
             *[pltpu.VMEM((2, 2, 2 * n, k), BF16) for n, k in zip(p.sizes, p.depths)],
             *[pltpu.VMEM((2, n, radix), F32) for n in p.sizes],
             *[pltpu.VMEM((2, 2, p.share, n, radix), F32) for n in p.sizes],
@@ -572,25 +674,25 @@
             pltpu.VMEM((p.comp, p.share, 2 * p.outs, radix), BF16),
             pltpu.VMEM((p.comp - 1, p.share, 2 * p.outs, radix), BF16),
             dma((PIECES,)),
-            dma((4,)),
-            dma((len(p.table_peers),)),
-            dma((len(p.table_peers),)),
+            dma((8,)),
+            dma((3 * p.comp,)),
+            dma((p.comp + 1,)),
             dma((units * (p.comp - 1),)),
             dma((units * (p.comp - 1),)),
-            dma((units * (p.beam - 1),)),
-            dma((units * (p.beam - 1),)),
-            dma((p.groups * len(p.swap_peers),)),
-            dma((p.groups * len(p.swap_peers),)),
-            dma((2 * p.groups,)),
-            dma((2 * p.groups,)),
+            dma((units * p.stages,)),
+            dma((units * p.stages,)),
+            dma((swap_count * len(p.swap_peers),)),
+            dma((swap_count * len(p.swap_peers),)),
+            dma((2 * swap_count,)),
+            dma((2 * swap_count,)),
             dma(((p.comp - 1) * OUT_PIECES,)),
             dma(((p.comp - 1) * OUT_PIECES,)),
         ],
         compiler_params=pltpu.CompilerParams(
-            collective_id=0, has_side_effects=True, vmem_limit_bytes=58 * 2**20
+            collective_id=0, has_side_effects=True, vmem_limit_bytes=LIMIT
         ),
     )(
-        angle, raw, filt, table, jnp.asarray(constants.T), jnp.asarray(constants.T),
+        angle, raw, filt, weights, offsets, delay, jnp.asarray(constants.T), jnp.asarray(constants.T),
         jnp.asarray(twiddle(radix)),
     )
 
@@ -600,19 +702,11 @@
     columns = band_offsets.shape[1]
     plan = Plan(counts, steer_angle.shape, raw_pulses.shape[2], columns)
     radix = plan.radix
-    table = jnp.concatenate(
-        [
-            band_weights.transpose(2, 0, 1).reshape(BAND, 2 * columns),
-            band_offsets.astype(F32).reshape(1, 2 * columns),
-            beam_delay.reshape(1, 2 * columns),
-        ],
-        axis=0,
+    filt = range_filter.reshape(2, radix, radix).transpose(1, 0, 2).reshape(2 * radix, radix)
+    out = fused(
+        plan, steer_angle, raw_pulses, filt, band_weights.transpose(0, 2, 1), band_offsets, beam_delay
     )
-    table = jnp.pad(
-        table, ((0, FIELDS - table.shape[0]), (0, plan.padded - 2 * columns))
-    )
-    filt = range_filter.reshape(2, radix, radix).transpose(1, 0, 2).reshape(2 * radix, radix)
-    out = fused(plan, steer_angle, raw_pulses, filt, table)
+    out = store(out)
     out = out.reshape(plan.outs, plan.quarter, 2, radix).transpose(0, 2, 1, 3)
     return out.reshape(plan.outs, 2, plan.quarter * radix)
 

time: 92.1 us -> 81.8 us (0.89)
  Pallas kernels: 86.6 us -> 81.5 us
  local copies, waits for them, and re-layouts: 3.93 us -> 0 us
  other arithmetic: 1.29 us -> 0 us
    pallas_call x1 -> x2, Pallas kernels: 86.6 us -> 81.5 us  [the longest x1 80.5 us: fused(): pl.pallas_call(functools.partial(fused_kernel, p), out_shape=pltpu.VMEM((...]
    unnamed x1 -> x0, local copies, waits for them, and re-layouts: 2.31 us -> none
    reshape x3 -> x0, local copies, waits for them, and re-layouts: 0.92 us -> none  [the longest x1 0.76 us: body(): beam_delay.reshape(1, 2 * columns)]
where the time goes in v2:
time: 81.8 us; the launch traced here: 81.7 us
  Pallas kernels  81.5 us (100%)
    pallas_call x1, Pallas kernels, fused(): pl.pallas_call(functools.partial(fused_kernel, p), out_shape=pltpu.VMEM((...  80.5 us

profile of v2, /device:TPU:0, one launch (start us, length us, event | category | flops | bytes accessed | tf_op | source)
XLA Modules:
  0.0 81.7 jit_solution(18349593768261251546)
XLA Ops:
  0.0 80.5 %shard_map.91.value_ref = f32[2048,128]{1,0:T(8,128)S(1)} custom-call(f32[64,128]{1,0:T(8,128)} %angle_hbm.1, bf16[128,2,16384]{2,1,0:T(2,128)(2,1)} %raw_hbm.1, f32[256,128]{1,0:T(8,128)} %bitcast.11, f32[2,8,48]{2,1,0:T(8,128)} %bitcast.12, s32[2,48]{1,0:T(2,128)} %offsets_hbm.1, f32[2,48]{1,0:T(2,128)} %delay_hbm.1, ...), custom_call_target="tpu_custom_call" | custom-call | tf_op jit(solution)/shard_map/pallas_call | solution.py:643
  80.5 1.0 %shard_map.92 = f32[2048,128]{1,0:T(8,128)} custom-call(f32[2048,128]{1,0:T(8,128)S(1)} %shard_map.91.value_ref), custom_call_target="tpu_custom_call" | custom-call | tf_op jit(solution)/shard_map/pallas_call | solution.py:625

commit v3 on v2

--- a/solution.py
+++ b/solution.py
@@ -14,11 +14,13 @@
 EXTRA = 8
 SIDE = 12
 GROUP = 2
-PIECES = 8
-LAG = 4
-LAG_TWO = 3
+PIECES = 4
+LAG = 3
+LAG_TWO = 2
+LAST_PIECES = 4
+BEAM_FIRST = (1, 5)
 OUT_PIECES = 4
-HALO_LAG = 4
+HALO_LAG = 2
 LIMIT = 54 * 2**20
 STORES = 4
 MESH = pl.DeviceIdType.MESH
@@ -68,7 +70,9 @@
         self.group = min(GROUP, self.first)
         self.groups = self.first // self.group
         self.rows = 2 * self.group
-        self.width = length // PIECES
+        self.counts = [PIECES] * (self.groups - 1) + [LAST_PIECES]
+        self.units = [(g, h) for g in range(self.groups) for h in range(self.counts[g])]
+        self.beam_first = [self.units[i] for i in BEAM_FIRST]
         self.levels = self.sub.bit_length() - 1
         self.quarter = self.radix // self.sub
         self.share = self.quarter // self.comp
@@ -118,6 +122,8 @@
         return taken
 
     held, recv_two = take(p.stages), take(p.stages)
+    wide_held, wide_recv = take(p.stages), take(p.stages)
+    late_held, late_recv = take(2)
     lhs, delay, phase = take(levels), take(levels), take(levels)
     (final, outbound, inbound, load_sem, const_sem, table_send, table_recv, one_send, one_recv,
      two_send, two_recv, swap_send, swap_recv, halo_send, halo_recv, out_send, out_recv) = rest
@@ -143,9 +149,13 @@
 
     angle_load = pltpu.make_async_copy(angle_hbm, angle_ref, const_sem.at[7])
     angle_load.start()
+    def columns_of(g, h):
+        width = p.length // p.counts[g]
+        return pl.ds(h * width, width)
+
     loads = []
     for h in range(PIECES):
-        cols = pl.ds(h * p.width, p.width)
+        cols = columns_of(0, h)
         loads.append(
             pltpu.make_async_copy(raw_hbm.at[:, :, cols], raw.at[:, :, cols], load_sem.at[h])
         )
@@ -206,18 +216,6 @@
     order = jnp.where(origin == source, 1.0, 0.0).astype(BF16)
     weight[...] = dot(order, dot(stacked, spread).astype(BF16)).astype(BF16)
 
-    pl.semaphore_wait(barrier, len(p.peers))
-
-    for copy in constants[:3]:
-        copy.wait()
-    mine[...] = jnp.zeros(mine.shape, F32)
-    for side in range(2):
-        row = side * SIDE
-        mine[row : row + BAND, : p.columns] = weights_ref[side]
-        mine[row + BAND : row + BAND + 1, : p.columns] = offsets_ref[side : side + 1].astype(F32)
-        mine[row + BAND + 1 : row + BAND + 2, : p.columns] = delay_ref[side : side + 1]
-    tables[1 + c] = mine[...]
-
     def table_copy(db, dc):
         slot = 1 + c if db == 0 else (0 if db > 0 else p.comp + 1)
         k = (db + 1) * p.comp + dc
@@ -235,12 +233,19 @@
             for e in range(p.comp):
                 action(table_copy(-1, e))
 
-    for e in range(1, p.comp):
-        table_copy(0, e).start()
-    table_ends(lambda copy: copy.start())
-
-    def columns_of(h):
-        return pl.ds(h * p.width, p.width)
+    def send_tables():
+        for copy in constants[:3]:
+            copy.wait()
+        mine[...] = jnp.zeros(mine.shape, F32)
+        for side in range(2):
+            row = side * SIDE
+            mine[row : row + BAND, : p.columns] = weights_ref[side]
+            mine[row + BAND : row + BAND + 1, : p.columns] = offsets_ref[side : side + 1].astype(F32)
+            mine[row + BAND + 1 : row + BAND + 2, : p.columns] = delay_ref[side : side + 1]
+        tables[1 + c] = mine[...]
+        for e in range(1, p.comp):
+            table_copy(0, e).start()
+        table_ends(lambda copy: copy.start())
 
     one, two, swaps = {}, {}, {}
 
@@ -249,56 +254,110 @@
 
     def form(h):
         loads[h].wait()
-        pulses = raw[:, :, columns_of(h)].reshape(-1, p.width)
-        product = dot(weight[...], pulses)
-        part[:, :, :, :, columns_of(h)] = product.astype(BF16).reshape(
-            p.groups, p.comp, p.beam, p.rows, p.width
-        )
+        cols = columns_of(0, h)
+        pulses = raw[:, :, cols].reshape(2 * p.pulses, -1)
+        product = dot(weight[...], pulses).astype(BF16)
+        part[:, :, :, :, :, cols] = product.reshape(
+            p.groups, p.comp, p.beam // 2, 2, p.rows, -1
+        )
+
+    def partner(stage):
+        return {"beam": b + (1 - 2 * bit(stage)) * 2**stage}
 
     def start_one(g, h):
+        if (g, h) in p.beam_first:
+            n = p.beam_first.index((g, h))
+            return send_wide(0, n, part.at[g, :, :, 1 - bit(0), :, columns_of(g, h)])
         one[g, h] = []
         for d in range(1, p.comp):
             peer = lax.rem(c + d, p.comp)
-            k = (g * PIECES + h) * (p.comp - 1) + d - 1
+            k = p.units.index((g, h)) * (p.comp - 1) + d - 1
             copy = remote(
-                part.at[g, peer, :, :, columns_of(h)],
-                recv_one.at[d - 1, g, :, :, columns_of(h)],
+                part.at[g, peer, :, :, :, columns_of(g, h)],
+                recv_one.at[d - 1, g, :, :, :, columns_of(g, h)],
                 one_send.at[k], one_recv.at[k], at(0, 0, d),
             )
             copy.start()
             one[g, h].append(copy)
 
+    def send_wide(stage, n, source):
+        k = p.units.index(p.beam_first[n]) * p.stages + stage
+        copy = remote(
+            source, wide_recv[stage].at[n], two_send.at[k], two_recv.at[k], partner(stage)
+        )
+        copy.start()
+        two[(stage,) + p.beam_first[n]] = copy
+
+    def gathered_wide(stage, n):
+        g, h = p.beam_first[n]
+        two[stage, g, h].wait_recv()
+        if stage == 0:
+            total = part[g, :, :, bit(0), :, columns_of(g, h)].astype(F32)
+        else:
+            total = wide_held[stage][n, :, :, bit(stage)].astype(F32)
+        return total + wide_recv[stage][n].astype(F32)
+
+    def step_wide(stage, n):
+        total = gathered_wide(stage - 1, n)
+        if stage < p.stages:
+            wide_held[stage][n] = total.astype(BF16).reshape(wide_held[stage].shape[1:])
+            return send_wide(stage, n, wide_held[stage].at[n, :, :, 1 - bit(stage)])
+        g, h = p.beam_first[n]
+        late_held[n] = total[:, 0].astype(BF16)
+        one[g, h] = []
+        for d in range(1, p.comp):
+            k = p.units.index((g, h)) * (p.comp - 1) + d - 1
+            copy = remote(
+                late_held.at[n, lax.rem(c + d, p.comp)], late_recv.at[n, d - 1],
+                one_send.at[k], one_recv.at[k], at(0, 0, d),
+            )
+            copy.start()
+            one[g, h].append(copy)
+
     def send_two(stage, g, h, total):
-        held[stage][g, :, :, :, columns_of(h)] = total.astype(BF16).reshape(
-            -1, 2, p.rows, p.width
-        )
-        k = (g * PIECES + h) * p.stages + stage
+        cols = columns_of(g, h)
+        held[stage][g, :, :, :, cols] = total.astype(BF16).reshape(-1, 2, p.rows, cols.size)
+        k = p.units.index((g, h)) * p.stages + stage
         copy = remote(
-            held[stage].at[g, :, 1 - bit(stage), :, columns_of(h)],
-            recv_two[stage].at[g, :, :, columns_of(h)],
-            two_send.at[k], two_recv.at[k],
-            {"beam": b + (1 - 2 * bit(stage)) * 2**stage},
+            held[stage].at[g, :, 1 - bit(stage), :, cols],
+            recv_two[stage].at[g, :, :, cols],
+            two_send.at[k], two_recv.at[k], partner(stage),
         )
         copy.start()
         two[stage, g, h] = copy
 
-    def start_two(g, h):
+    def gathered(stage, g, h):
+        cols = columns_of(g, h)
+        two[stage, g, h].wait_recv()
+        total = held[stage][g, :, bit(stage), :, cols].astype(F32)
+        return total + recv_two[stage][g, :, :, cols].astype(F32)
+
+    def step_beam(stage, g, h):
+        if (g, h) in p.beam_first:
+            return step_wide(stage + 1, p.beam_first.index((g, h)))
+        if stage > 0:
+            return send_two(stage, g, h, gathered(stage - 1, g, h))
+        cols = columns_of(g, h)
         for copy in one[g, h]:
             copy.wait_recv()
-        total = part[g, c, :, :, columns_of(h)].astype(F32)
+        total = part[g, c, :, :, :, cols].astype(F32)
         for d in range(1, p.comp):
-            total += recv_one[d - 1, g, :, :, columns_of(h)].astype(F32)
+            total += recv_one[d - 1, g, :, :, :, cols].astype(F32)
         send_two(0, g, h, total)
 
-    def gathered(stage, g, h):
-        two[stage, g, h].wait_recv()
-        total = held[stage][g, :, bit(stage), :, columns_of(h)].astype(F32)
-        return total + recv_two[stage][g, :, :, columns_of(h)].astype(F32)
-
     def finish(g, h):
-        total = gathered(p.stages - 1, g, h)[0]
-        for a in range(p.width // radix):
-            swap[pl.ds(h * (p.width // radix) + a, p.rows, stride=radix), :] = total[
+        if (g, h) in p.beam_first:
+            n = p.beam_first.index((g, h))
+            total = late_held[n, c].astype(F32)
+            for copy in one[g, h]:
+                copy.wait_recv()
+            for d in range(1, p.comp):
+                total += late_recv[n, d - 1].astype(F32)
+        else:
+            total = gathered(p.stages - 1, g, h)[0]
+        width = p.length // p.counts[g]
+        for a in range(width // radix):
+            swap[pl.ds(h * (width // radix) + a, p.rows, stride=radix), :] = total[
                 :, a * radix : (a + 1) * radix
             ]
 
@@ -511,27 +570,29 @@
             value = source[r * p.outs : (r + 1) * p.outs].astype(F32)
             out_ref[pl.ds(2 * (column * p.share + m) + r, p.outs, stride=2 * p.quarter), :] = value
 
-    units = [(g, h) for g in range(p.groups) for h in range(PIECES)]
+    units = p.units
     total_units = len(units)
     idle = range(PIECES, 2 * PIECES)
     per_step = -(-p.share // len(idle))
     pending = []
     last = p.groups - 1
     drain = LAG + LAG_TWO * p.stages
+    form(0)
+    pl.semaphore_wait(barrier, len(p.peers))
     for u in range(total_units + drain):
-        if u < PIECES:
+        if 0 < u < PIECES:
             form(u)
         if u < total_units:
             start_one(*units[u])
+        if u == 1:
+            send_tables()
         if u == total_units - 1:
             for copy in deferred:
                 copy.start()
-        if 0 <= u - LAG < total_units:
-            start_two(*units[u - LAG])
-        for stage in range(1, p.stages):
+        for stage in range(p.stages):
             v = u - LAG - LAG_TWO * stage
             if 0 <= v < total_units:
-                send_two(stage, *units[v], gathered(stage - 1, *units[v]))
+                step_beam(stage, *units[v])
         v = u - drain
         while pending and v >= pending[0][0]:
             start_halo(pending.pop(0)[1])
@@ -549,8 +610,8 @@
         if v >= 0:
             finish(*units[v])
             g, h = units[v]
-            if h == PIECES - 1:
-                compress(g, u < total_units)
+            if h == p.counts[g] - 1:
+                compress(g, u < total_units - 1)
                 if g < last:
                     pending.append((max(v + HALO_LAG, total_units - drain + 4), g))
     for _, g in pending:
@@ -637,7 +698,9 @@
     constants = real_form(p.radix)
     dma = pltpu.SemaphoreType.DMA
     radix = p.radix
-    units = p.groups * PIECES
+    units = len(p.units)
+    wide = p.length // PIECES
+    early = len(p.beam_first)
     halves = [p.beam // 2 ** (t + 1) for t in range(p.stages)]
     swap_count = p.groups - 1 + OUT_PIECES
     return pl.pallas_call(
@@ -652,8 +715,8 @@
             pltpu.VMEM(delay.shape, F32),
             pltpu.VMEM(raw.shape, BF16),
             pltpu.VMEM((2 * p.beams, 2 * p.pulses), BF16),
-            pltpu.VMEM((p.groups, p.comp, p.beam, p.rows, p.length), BF16),
-            pltpu.VMEM((p.comp - 1, p.groups, p.beam, p.rows, p.length), BF16),
+            pltpu.VMEM((p.groups, p.comp, p.beam // 2, 2, p.rows, p.length), BF16),
+            pltpu.VMEM((p.comp - 1, p.groups, p.beam // 2, 2, p.rows, p.length), BF16),
             pltpu.VMEM((p.rows * radix, radix), F32),
             pltpu.VMEM((2 * radix, 2 * radix), BF16),
             pltpu.VMEM((2 * radix, 2 * radix), BF16),
@@ -667,6 +730,13 @@
             pltpu.VMEM((p.padded, 128), F32),
             *[pltpu.VMEM((p.groups, n, 2, p.rows, p.length), BF16) for n in halves],
             *[pltpu.VMEM((p.groups, n, p.rows, p.length), BF16) for n in halves],
+            *[
+                pltpu.VMEM((early, p.comp, n if t else 1, 2, p.rows, wide if t else 128), BF16)
+                for t, n in enumerate(halves)
+            ],
+            *[pltpu.VMEM((early, p.comp, n, p.rows, wide), BF16) for n in halves],
+            pltpu.VMEM((early, p.comp, p.rows, wide), BF16),
+            pltpu.VMEM((early, p.comp - 1, p.rows, wide), BF16),
             *[pltpu.VMEM((2, 2, 2 * n, k), BF16) for n, k in zip(p.sizes, p.depths)],
             *[pltpu.VMEM((2, n, radix), F32) for n in p.sizes],
             *[pltpu.VMEM((2, 2, p.share, n, radix), F32) for n in p.sizes],

time: 81.8 us -> 75.1 us (0.918)
  Pallas kernels: 81.5 us -> 74.9 us
    pallas_call x1, Pallas kernels: 80.5 us -> 73.9 us  [fused(): pl.pallas_call(functools.partial(fused_kernel, p), out_shape=pltpu.VMEM((...]
where the time goes in v3:
time: 75.1 us; the launch traced here: 74.9 us
  Pallas kernels  74.9 us (100%)
    pallas_call x1, Pallas kernels, fused(): pl.pallas_call(functools.partial(fused_kernel, p), out_shape=pltpu.VMEM((...  73.9 us

profile of v3, /device:TPU:0, one launch (start us, length us, event | category | flops | bytes accessed | tf_op | source)
XLA Modules:
  0.0 74.9 jit_solution(1138366876308413682)
XLA Ops:
  0.0 73.9 %shard_map.91.value_ref = f32[2048,128]{1,0:T(8,128)S(1)} custom-call(f32[64,128]{1,0:T(8,128)} %angle_hbm.1, bf16[128,2,16384]{2,1,0:T(2,128)(2,1)} %raw_hbm.1, f32[256,128]{1,0:T(8,128)} %bitcast.11, f32[2,8,48]{2,1,0:T(8,128)} %bitcast.12, s32[2,48]{1,0:T(2,128)} %offsets_hbm.1, f32[2,48]{1,0:T(2,128)} %delay_hbm.1, ...), custom_call_target="tpu_custom_call" | custom-call | tf_op jit(solution)/shard_map/pallas_call | solution.py:706
  73.9 1.0 %shard_map.92 = f32[2048,128]{1,0:T(8,128)} custom-call(f32[2048,128]{1,0:T(8,128)S(1)} %shard_map.91.value_ref), custom_call_target="tpu_custom_call" | custom-call | tf_op jit(solution)/shard_map/pallas_call | solution.py:686

commit v4 on v3

--- a/solution.py
+++ b/solution.py
@@ -18,7 +18,7 @@
 LAG = 3
 LAG_TWO = 2
 LAST_PIECES = 4
-BEAM_FIRST = (1, 5)
+BEAM_FIRST = (1, 4, 7, 10)
 OUT_PIECES = 4
 HALO_LAG = 2
 LIMIT = 54 * 2**20

time: 75.1 us -> 71.7 us (0.955)
  Pallas kernels: 74.9 us -> 71.5 us
    pallas_call x1, Pallas kernels: 73.9 us -> 70.5 us  [fused(): pl.pallas_call(functools.partial(fused_kernel, p), out_shape=pltpu.VMEM((...]
where the time goes in v4:
time: 71.7 us; the launch traced here: 71.6 us
  Pallas kernels  71.5 us (100%)
    pallas_call x1, Pallas kernels, fused(): pl.pallas_call(functools.partial(fused_kernel, p), out_shape=pltpu.VMEM((...  70.5 us

profile of v4, /device:TPU:0, one launch (start us, length us, event | category | flops | bytes accessed | tf_op | source)
XLA Modules:
  0.0 71.6 jit_solution(9991907028052145914)
XLA Ops:
  0.0 70.5 %shard_map.91.value_ref = f32[2048,128]{1,0:T(8,128)S(1)} custom-call(f32[64,128]{1,0:T(8,128)} %angle_hbm.1, bf16[128,2,16384]{2,1,0:T(2,128)(2,1)} %raw_hbm.1, f32[256,128]{1,0:T(8,128)} %bitcast.11, f32[2,8,48]{2,1,0:T(8,128)} %bitcast.12, s32[2,48]{1,0:T(2,128)} %offsets_hbm.1, f32[2,48]{1,0:T(2,128)} %delay_hbm.1, ...), custom_call_target="tpu_custom_call" | custom-call | tf_op jit(solution)/shard_map/pallas_call | solution.py:706
  70.6 1.0 %shard_map.92 = f32[2048,128]{1,0:T(8,128)} custom-call(f32[2048,128]{1,0:T(8,128)S(1)} %shard_map.91.value_ref), custom_call_target="tpu_custom_call" | custom-call | tf_op jit(solution)/shard_map/pallas_call | solution.py:686

commit v5 on v4

--- a/solution.py
+++ b/solution.py
@@ -18,7 +18,7 @@
 LAG = 3
 LAG_TWO = 2
 LAST_PIECES = 4
-BEAM_FIRST = (1, 4, 7, 10)
+BEAM_FIRST = (1, 4, 7, 11)
 OUT_PIECES = 4
 HALO_LAG = 2
 LIMIT = 54 * 2**20

time: 71.7 us -> 70.8 us (0.987)
  Pallas kernels: 71.5 us -> 70.6 us
    pallas_call x1, Pallas kernels: 70.5 us -> 69.6 us  [fused(): pl.pallas_call(functools.partial(fused_kernel, p), out_shape=pltpu.VMEM((...]
where the time goes in v5:
time: 70.8 us; the launch traced here: 70.6 us
  Pallas kernels  70.6 us (100%)
    pallas_call x1, Pallas kernels, fused(): pl.pallas_call(functools.partial(fused_kernel, p), out_shape=pltpu.VMEM((...  69.6 us

profile of v5, /device:TPU:0, one launch (start us, length us, event | category | flops | bytes accessed | tf_op | source)
XLA Modules:
  0.0 70.6 jit_solution(14885069965615774834)
XLA Ops:
  0.0 69.6 %shard_map.91.value_ref = f32[2048,128]{1,0:T(8,128)S(1)} custom-call(f32[64,128]{1,0:T(8,128)} %angle_hbm.1, bf16[128,2,16384]{2,1,0:T(2,128)(2,1)} %raw_hbm.1, f32[256,128]{1,0:T(8,128)} %bitcast.11, f32[2,8,48]{2,1,0:T(8,128)} %bitcast.12, s32[2,48]{1,0:T(2,128)} %offsets_hbm.1, f32[2,48]{1,0:T(2,128)} %delay_hbm.1, ...), custom_call_target="tpu_custom_call" | custom-call | tf_op jit(solution)/shard_map/pallas_call | solution.py:706
  69.6 1.0 %shard_map.92 = f32[2048,128]{1,0:T(8,128)} custom-call(f32[2048,128]{1,0:T(8,128)S(1)} %shard_map.91.value_ref), custom_call_target="tpu_custom_call" | custom-call | tf_op jit(solution)/shard_map/pallas_call | solution.py:686

commit v6 on v5

--- a/solution.py
+++ b/solution.py
@@ -20,7 +20,7 @@
 LAST_PIECES = 4
 BEAM_FIRST = (1, 4, 7, 11)
 OUT_PIECES = 4
-HALO_LAG = 2
+HALO_LAG = 1
 LIMIT = 54 * 2**20
 STORES = 4
 MESH = pl.DeviceIdType.MESH
@@ -96,7 +96,10 @@
         need = min(need, self.first) if self.comp > 1 else self.first
         self.edges = [g for g in range(self.groups) if g * self.group < need]
         self.swap_peers = [
-            (d, e) for d in range(self.sub) for e in range(self.comp) if (d, e) != (0, 0)
+            (d, e)
+            for d in reversed(range(self.sub))
+            for e in reversed(range(self.comp))
+            if (d, e) != (0, 0)
         ]
 
     def pieces(self, level):

time: 70.8 us -> 70.9 us (level)
  no operation moved by 1% of the time
where the time goes in v6:
time: 70.9 us; the launch traced here: 70.7 us
  Pallas kernels  70.7 us (100%)
    pallas_call x1, Pallas kernels, fused(): pl.pallas_call(functools.partial(fused_kernel, p), out_shape=pltpu.VMEM((...  69.7 us

profile of v6, /device:TPU:0, one launch (start us, length us, event | category | flops | bytes accessed | tf_op | source)
XLA Modules:
  0.0 70.7 jit_solution(1517564486444504613)
XLA Ops:
  0.0 69.7 %shard_map.91.value_ref = f32[2048,128]{1,0:T(8,128)S(1)} custom-call(f32[64,128]{1,0:T(8,128)} %angle_hbm.1, bf16[128,2,16384]{2,1,0:T(2,128)(2,1)} %raw_hbm.1, f32[256,128]{1,0:T(8,128)} %bitcast.11, f32[2,8,48]{2,1,0:T(8,128)} %bitcast.12, s32[2,48]{1,0:T(2,128)} %offsets_hbm.1, f32[2,48]{1,0:T(2,128)} %delay_hbm.1, ...), custom_call_target="tpu_custom_call" | custom-call | tf_op jit(solution)/shard_map/pallas_call | solution.py:709
  69.7 1.0 %shard_map.92 = f32[2048,128]{1,0:T(8,128)} custom-call(f32[2048,128]{1,0:T(8,128)S(1)} %shard_map.91.value_ref), custom_call_target="tpu_custom_call" | custom-call | tf_op jit(solution)/shard_map/pallas_call | solution.py:689
